TPU v7x, 512 devices: a whole 4x4x16 slice. The times are simulated.
512 devices in a mesh: ctx: 64 (over z, y), dp: 8 (over x, core).
Axes of the slice: x: 4, y: 4, z: 16, core: 2. Of those that a mesh axis runs over, the one named last changes fastest.
Arguments:
- q_in: bfloat16 [8, 8192, 2048], P('dp', 'ctx'), may hold values from -6 to 6
- k_in: bfloat16 [8, 8192, 2048], P('dp', 'ctx'), may hold values from -6 to 6
- v_in: bfloat16 [8, 8192, 2048], P('dp', 'ctx'), may hold values from -6 to 6
- grad_out: bfloat16 [8, 8192, 2048], P('dp', 'ctx'), may hold values from -6 to 6
- short_filter: float32 [3, 3, 2048], replicated, may hold values from -3.5 to 3.5
- residue: float32 [2048, 8], replicated, may hold values from -2 to 2
- rate: float32 [8], replicated, may hold values from 0.00012207031 to 0.1
Outputs:
- mixed: bfloat16 [8, 8192, 2048], P('dp', 'ctx')
- grad_q: bfloat16 [8, 8192, 2048], P('dp', 'ctx')
- grad_k: bfloat16 [8, 8192, 2048], P('dp', 'ctx')
- grad_v: bfloat16 [8, 8192, 2048], P('dp', 'ctx')
- grad_residue: float32 [2048, 8], P('ctx')
- grad_short: float32 [3, 3, 2048], replicated
All inputs are finite; a program needn't handle non-finite values.
Results may differ from a plain program's by a relative error of at most 0.024.
Values may be sent and summed in bfloat16 or wider, within the bound.
A program may use at most 64 MiB of HBM per device.

v0:
```python
import jax
import jax.numpy as jnp
from jax import lax
from jax.sharding import PartitionSpec as P

BLOCK = 128


PRECISE = lax.Precision.HIGHEST


def passed_along(block, axis, distance):
    devices = range(lax.axis_size(axis))
    route = [(i - distance, i) for i in devices if i - distance in devices]
    return lax.ppermute(block, axis, route)


def mode_sweeps(source, cotangent, rates, columns, gains, front, behind):
    block_len = BLOCK
    block_count = source.shape[1]
    places = jnp.arange(block_len, dtype=jnp.float32)
    offset = places[:, None] - places[None, :]
    blocks = jnp.arange(block_count, dtype=jnp.float32)
    spacing = blocks[:, None] - blocks[None, :] - 1.0
    cot_f = cotangent.astype(jnp.float32)

    def one_mode(carry, item):
        conv_acc, back_acc = carry
        speed, column, start_fwd, start_back = item
        kernel = jnp.where(offset >= 0, jnp.exp(-speed * jnp.maximum(offset, 0.0)), 0.0).astype(
            jnp.bfloat16
        )
        passing = jnp.where(
            spacing >= 0, jnp.exp(-speed * block_len * jnp.maximum(spacing, 0.0)), 0.0
        )
        lead = jnp.exp(-speed * block_len * blocks)
        trail = jnp.exp(-speed * block_len * (block_count - 1.0 - blocks))
        scale_fwd = jnp.exp(-speed * (places + 1.0))
        scale_back = jnp.exp(-speed * (block_len - places))
        inside = jnp.einsum("ts,cns->cnt", kernel, source, preferred_element_type=jnp.float32)
        entering = (
            jnp.einsum("nk,ck->cn", passing, inside[..., block_len - 1], precision=PRECISE)
            + lead[None, :] * start_fwd[:, None]
        )
        forward = inside + scale_fwd[None, None, :] * entering[..., None]
        conv_acc = conv_acc + column[:, None, None] * forward
        grad_row = jnp.sum(forward * cot_f, axis=(1, 2))
        inside_back = jnp.einsum(
            "ts,cnt->cns", kernel, cotangent, preferred_element_type=jnp.float32
        )
        entering_back = (
            jnp.einsum("kn,ck->cn", passing, inside_back[..., 0], precision=PRECISE)
            + trail[None, :] * start_back[:, None]
        )
        backward = inside_back + scale_back[None, None, :] * entering_back[..., None]
        back_acc = back_acc + column[:, None, None] * backward
        return ((conv_acc, back_acc), grad_row)

    zeros_acc = jnp.zeros(source.shape, jnp.float32)
    (conv_sum, back_sum), grads = lax.scan(
        one_mode, (zeros_acc, zeros_acc), (rates, columns, front, behind)
    )
    grads = gains[:, None] * grads
    return (conv_sum, back_sum, grads.T)


def shards(q_in, k_in, v_in, grad_out, short_filter, residue, rate):
    row_count = q_in.shape[1]
    width = q_in.shape[2]
    inputs = (q_in[0], k_in[0], v_in[0])
    tails = jnp.stack([item[row_count - 2 :] for item in inputs])
    before = passed_along(tails, "ctx", 1)
    extended = [
        jnp.concatenate([before[branch], inputs[branch]], axis=0).astype(jnp.float32)
        for branch in range(3)
    ]
    shorts = []
    for branch in range(3):
        total = short_filter[branch, 0][None, :] * extended[branch][2 : 2 + row_count]
        for tap_at in range(1, 3):
            total = (
                total
                + short_filter[branch, tap_at][None, :]
                * extended[branch][2 - tap_at : 2 - tap_at + row_count]
            )
        shorts.append(total)
    query, keyed, valued = shorts
    gated = (keyed * valued).astype(jnp.bfloat16)
    cot_out = grad_out[0].astype(jnp.float32)
    d_conv = (cot_out * query).astype(jnp.bfloat16)
    gains = jnp.sqrt(1.0 - jnp.exp(-2.0 * rate))
    weights = residue * gains[None, :]
    modes = rate.shape[0]
    ctx_count = lax.axis_size("ctx")
    channel_share = width // ctx_count
    owned, incoming = (
        lax.all_to_all(gated, "ctx", split_axis=1, concat_axis=0, tiled=True),
        lax.all_to_all(d_conv, "ctx", split_axis=1, concat_axis=0, tiled=True),
    )
    total_rows = owned.shape[0]
    block_count = total_rows // BLOCK
    owned_lanes = owned.T.reshape(channel_share, block_count, BLOCK)
    incoming_lanes = incoming.T.reshape(channel_share, block_count, BLOCK)
    columns = lax.dynamic_slice_in_dim(
        weights, lax.axis_index("ctx") * channel_share, channel_share, 0
    ).T
    zero_start = jnp.zeros((modes, channel_share), jnp.float32)
    conv_sum, back_sum, partial_value = mode_sweeps(
        owned_lanes, incoming_lanes, rate, columns, gains, zero_start, zero_start
    )
    conv_rows = conv_sum.reshape(channel_share, total_rows).T.astype(jnp.bfloat16)
    back_rows = back_sum.reshape(channel_share, total_rows).T.astype(jnp.bfloat16)
    conv, d_gated = (
        lax.all_to_all(conv_rows, "ctx", split_axis=0, concat_axis=1, tiled=True),
        lax.all_to_all(back_rows, "ctx", split_axis=0, concat_axis=1, tiled=True),
    )
    grad_residue = lax.psum(partial_value, "dp")
    conv_f = conv.astype(jnp.float32)
    mixed = (query * conv_f).astype(jnp.bfloat16)
    gated_back = d_gated.astype(jnp.float32)
    d_shorts = (cot_out * conv_f, gated_back * valued, gated_back * keyed)
    heads = jnp.stack([item[:2] for item in d_shorts])
    after = passed_along(heads.astype(jnp.bfloat16), "ctx", -1).astype(heads.dtype)
    grads = []
    partial_short = []
    for branch in range(3):
        ahead_rows = jnp.concatenate([d_shorts[branch], after[branch]], axis=0)
        total = short_filter[branch, 0][None, :] * ahead_rows[0:row_count]
        for tap_at in range(1, 3):
            total = (
                total
                + short_filter[branch, tap_at][None, :] * ahead_rows[tap_at : tap_at + row_count]
            )
        grads.append(total.astype(jnp.bfloat16)[None])
        partial_short.append(
            jnp.stack(
                [
                    jnp.sum(
                        d_shorts[branch] * extended[branch][2 - tap_at : 2 - tap_at + row_count],
                        axis=0,
                    )
                    for tap_at in range(3)
                ]
            )
        )
    grad_short = lax.psum(jnp.stack(partial_short), ("ctx", "dp"))
    return (mixed[None], grads[0], grads[1], grads[2], grad_residue, grad_short)


def solution(mesh):
    placed = (
        P("dp", "ctx", None),
        P("dp", "ctx", None),
        P("dp", "ctx", None),
        P("dp", "ctx", None),
        P(),
        P(),
        P(),
    )
    return jax.shard_map(
        shards,
        mesh=mesh,
        in_specs=placed,
        out_specs=(
            P("dp", "ctx", None),
            P("dp", "ctx", None),
            P("dp", "ctx", None),
            P("dp", "ctx", None),
            P("ctx", None),
            P(),
        ),
        check_vma=False,
    )
```

profile of v0, /device:TPU:1, one launch (start us, length us, event | category | flops | bytes accessed | tf_op | source)
XLA Modules:
  0.0 703.1 jit_solution(16576350189797462453)
XLA Ops:
  9.5 4.0 collective-permute-start
  18.7 4.5 multiply_convert_fusion
  23.2 18.3 %all-to-all-start = ((bf16[128,64,32]{0,2,1:T(8,128)(2,1)}), bf16[128,64,32]{0,2,1:T(8,128)(2,1)S(1)}, u32[]{:S(2)}, u32[]{:S(2)}) async-start(bf16[128,64,32]{0,2,1:T(8,128)(2,1)} %bitcast.16), calls=%async_computation | async-start | bytes 1048576 | tf_op jit(solution)/shard_map/all_to_all | solution.py:97
  44.2 2.4 fusion.51
  46.6 24.2 %all-to-all-done = bf16[128,64,32]{0,2,1:T(8,128)(2,1)S(1)} async-done(((bf16[128,64,32]{0,2,1:T(8,128)(2,1)}), bf16[128,64,32]{0,2,1:T(8,128)(2,1)S(1)}, u32[]{:S(2)}, u32[]{:S(2)}) %all-to-all-start) | async-done | bytes 524320 | tf_op jit(solution)/shard_map/all_to_all | solution.py:97
  70.7 8.6 %all-to-all-start.1 = ((bf16[128,64,32]{0,2,1:T(8,128)(2,1)}), bf16[128,64,32]{0,2,1:T(8,128)(2,1)S(1)}, u32[]{:S(2)}, u32[]{:S(2)}) async-start(bf16[128,64,32]{0,2,1:T(8,128)(2,1)} %bitcast.20), calls=%async_computation.1 | async-start | bytes 1048576 | tf_op jit(solution)/shard_map/all_to_all | solution.py:98
  81.2 27.1 %all-to-all-done.1 = bf16[128,64,32]{0,2,1:T(8,128)(2,1)S(1)} async-done(((bf16[128,64,32]{0,2,1:T(8,128)(2,1)}), bf16[128,64,32]{0,2,1:T(8,128)(2,1)S(1)}, u32[]{:S(2)}, u32[]{:S(2)}) %all-to-all-start.1) | async-done | bytes 524320 | tf_op jit(solution)/shard_map/all_to_all | solution.py:98
  110.5 60.8 %while.16 = (s32[]{:T(128)}, f32[32,64,128]{2,1,0:T(8,128)}, f32[32,64,128]{2,1,0:T(8,128)}, f32[8,32]{1,0:T(8,128)S(1)}, f32[8,32]{1,0:T(8,128)S(1)}, /*index=5...) while((s32[]{:T(128)}, f32[32,64,128]{2,1,0:T(8,128)}, ...), condition=%wide.region_2.3_spmd.clone.clone, body=%wide.region_0.2_spmd.clone.clone.sunk | while | flops 140759840 | bytes 12668891 | solution.py:60
  114.9 2.2 multiply_reduce_fusion.11
  121.5 3.3 multiply_reduce_fusion.11
  129.2 3.3 multiply_reduce_fusion.11
  133.8 1.4 convolution_bitcast_fusion.5
  137.0 3.3 multiply_reduce_fusion.11
  144.7 3.3 multiply_reduce_fusion.11
  152.5 3.3 multiply_reduce_fusion.11
  157.1 1.4 convolution_bitcast_fusion.5
  160.2 3.3 multiply_reduce_fusion.11
  164.8 1.4 convolution_bitcast_fusion.5
  167.9 3.3 multiply_reduce_fusion.11
  173.8 9.2 %all-to-all-start.3 = ((bf16[64,128,32]{1,2,0:T(8,128)(2,1)}), bf16[64,128,32]{1,2,0:T(8,128)(2,1)}, u32[]{:S(2)}, u32[]{:S(2)}) async-start(bf16[64,128,32]{1,2,0:T(8,128)(2,1)} %copy_bitcast_fusion), calls=%async_computation.3 | async-start | bytes 1048576 | tf_op jit(solution)/shard_map/all_to_all | solution.py:115
  184.3 27.9 %all-to-all-done.3 = bf16[64,128,32]{1,2,0:T(8,128)(2,1)} async-done(((bf16[64,128,32]{1,2,0:T(8,128)(2,1)}), bf16[64,128,32]{1,2,0:T(8,128)(2,1)}, u32[]{:S(2)}, u32[]{:S(2)}) %all-to-all-start.3) | async-done | bytes 524320 | tf_op jit(solution)/shard_map/all_to_all | solution.py:115
  212.1 8.9 %all-to-all-start.2 = ((bf16[64,128,32]{1,2,0:T(8,128)(2,1)}), bf16[64,128,32]{1,2,0:T(8,128)(2,1)}, u32[]{:S(2)}, u32[]{:S(2)}) async-start(bf16[64,128,32]{1,2,0:T(8,128)(2,1)} %copy_bitcast_fusion.1), calls=%async_computation.2 | async-start | bytes 1048576 | tf_op jit(solution)/shard_map/all_to_all | solution.py:114
  221.2 14.6 %psum.14 = f32[32,8]{0,1:T(8,128)} all-reduce(f32[32,8]{0,1:T(8,128)S(1)} %multiply_bitcast_fusion), channel_id=1, replica_groups=mesh['ctx'=64,'dp'=8] {'dp'}, use_global_device_ids=true, to_apply=%region_3.4 | all-reduce | flops 256 | bytes 2048 | tf_op jit(solution)/shard_map/psum | solution.py:117
  235.8 6.3 multiply_reduce_fusion.6
  247.3 2.9 all-to-all-done.2
  250.2 3.0 multiply_reduce_fusion.9
  256.6 1.5 collective-permute-done.1
  260.4 2.2 fusion.76
  262.6 2.2 fusion.75
  264.8 2.2 fusion.74
  270.0 424.7 %all-reduce.2.cloned.1.call-done = f32[3,3,2048]{2,1,0:T(4,128)} async-done(((f32[3,3,2048]{2,1,0:T(4,128)}), f32[3,3,2048]{2,1,0:T(4,128)}) %all-reduce.2.cloned.1.call-update) | async-done | bytes 73744 | tf_op jit(solution)/shard_map/psum | solution.py:146
  694.7 1.5 copy.80
  (183 shorter events, 57.1 us)
Async XLA Ops:
  9.5 7.7 %collective-permute-start = (bf16[3,2,2048]{2,1,0:T(2,128)(2,1)S(1)}, bf16[3,2,2048]{2,1,0:T(2,128)(2,1)S(1)}, u32[]{:S(2)}, u32[]{:S(2)}) collective-permute-start(bf16[3,2,2048]{2,1,0:T(2,128)(2,1)S(1)} %pad_maximum_fusion.4), channel_id=1, source_target_pairs={{0,8},{8,16},{16,24},{24,32},{32,40},{40,48},{48,56},{56,64},{64,7... | collective-permute-start | bytes 73736 | tf_op jit(solution)/shard_map/ppermute | solution.py:15
  18.7 4.5 copy-start.1
  18.7 4.5 copy-start.3
  18.7 22.8 %copy-start.13 = (bf16[1,128,2048]{2,1,0:T(8,128)(2,1)S(1)}, bf16[1,128,2048]{2,1,0:T(8,128)(2,1)}, u32[]{:S(2)}) copy-start(bf16[1,128,2048]{2,1,0:T(8,128)(2,1)} %param.9) | copy-start | bytes 1572868
  23.2 18.6 %copy-start.14 = (bf16[1,128,2048]{2,1,0:T(8,128)(2,1)S(1)}, bf16[1,128,2048]{2,1,0:T(8,128)(2,1)}, u32[]{:S(2)}) copy-start(bf16[1,128,2048]{2,1,0:T(8,128)(2,1)} %param.12) | copy-start | bytes 1572868
  23.2 47.5 %all-to-all-start = ((bf16[128,64,32]{0,2,1:T(8,128)(2,1)}), bf16[128,64,32]{0,2,1:T(8,128)(2,1)S(1)}, u32[]{:S(2)}, u32[]{:S(2)}) async-start(bf16[128,64,32]{0,2,1:T(8,128)(2,1)} %bitcast.16), calls=%async_computation | async-start | bytes 1048576 | tf_op jit(solution)/shard_map/all_to_all | solution.py:97
  42.1 4.5 copy-start.11
  42.8 1.4 copy-start.4
  44.2 35.2 %copy-start.15 = (f32[8]{0:T(128)S(1)}, f32[8]{0:T(128)}, u32[]{:S(2)}) copy-start(f32[8]{0:T(128)} %param.15) | copy-start | bytes 100
  70.7 37.6 %all-to-all-start.1 = ((bf16[128,64,32]{0,2,1:T(8,128)(2,1)}), bf16[128,64,32]{0,2,1:T(8,128)(2,1)S(1)}, u32[]{:S(2)}, u32[]{:S(2)}) async-start(bf16[128,64,32]{0,2,1:T(8,128)(2,1)} %bitcast.20), calls=%async_computation.1 | async-start | bytes 1048576 | tf_op jit(solution)/shard_map/all_to_all | solution.py:98
  111.7 2.0 copy-start.6
  118.3 2.0 copy-start.6
  126.1 2.0 copy-start.6
  133.8 2.0 copy-start.6
  141.6 2.0 copy-start.6
  149.3 2.0 copy-start.6
  157.0 2.0 copy-start.6
  164.8 2.0 copy-start.6
  171.3 11.8 %copy-start = (f32[32,64,128]{2,1,0:T(8,128)S(1)}, f32[32,64,128]{2,1,0:T(8,128)}, u32[]{:S(2)}) copy-start(f32[32,64,128]{2,1,0:T(8,128)} %get-tuple-element.87) | copy-start | bytes 3145732
  173.8 38.3 %all-to-all-start.3 = ((bf16[64,128,32]{1,2,0:T(8,128)(2,1)}), bf16[64,128,32]{1,2,0:T(8,128)(2,1)}, u32[]{:S(2)}, u32[]{:S(2)}) async-start(bf16[64,128,32]{1,2,0:T(8,128)(2,1)} %copy_bitcast_fusion), calls=%async_computation.3 | async-start | bytes 1048576 | tf_op jit(solution)/shard_map/all_to_all | solution.py:115
  183.0 52.7 %copy-start.2 = (f32[130,2048]{0,1:T(8,128)S(1)}, f32[130,2048]{0,1:T(8,128)}, u32[]{:S(2)}) copy-start(f32[130,2048]{0,1:T(8,128)} %copy-done.1) | copy-start | bytes 3194884
  212.1 38.0 %all-to-all-start.2 = ((bf16[64,128,32]{1,2,0:T(8,128)(2,1)}), bf16[64,128,32]{1,2,0:T(8,128)(2,1)}, u32[]{:S(2)}, u32[]{:S(2)}) async-start(bf16[64,128,32]{1,2,0:T(8,128)(2,1)} %copy_bitcast_fusion.1), calls=%async_computation.2 | async-start | bytes 1048576 | tf_op jit(solution)/shard_map/all_to_all | solution.py:114
  221.0 473.7 %all-reduce.2.cloned.1.call-start = ((), (), s32[]{:S(2)}) async-start(), calls=%async_computation.4 | async-start | bytes 196608 | tf_op jit(solution)/shard_map/psum | solution.py:146
  242.1 1.0 copy-start.7
  242.1 8.1 %copy-start.9 = (f32[128,2048]{0,1:T(8,128)}, f32[128,2048]{0,1:T(8,128)S(1)}, u32[]{:S(2)}) copy-start(f32[128,2048]{0,1:T(8,128)S(1)} %get-tuple-element.228) | copy-start | bytes 3145732
  242.1 8.0 %copy-start.5 = (f32[130,2048]{0,1:T(8,128)S(1)}, f32[130,2048]{0,1:T(8,128)}, u32[]{:S(2)}) copy-start(f32[130,2048]{0,1:T(8,128)} %copy-done.4) | copy-start | bytes 3194884
  253.2 2.4 copy-start.12
  253.5 4.6 collective-permute-start.1
  259.1 1.2 copy-start.10
  259.4 3.2 copy-start.8
Sparse Core Ops, SparseCore 0:
  255.7 438.9 all-reduce.1
where the time goes:
time: 705 us; the launch traced here: 703 us
  waiting for transfers between devices  508 us (72%)
  other arithmetic  54 us (8%)
  starting transfers between devices  50.4 us (7%)
  local copies, waits for them, and re-layouts  39.1 us (6%)
  matrix products  16.5 us (2%)
  blocking collectives  14.6 us (2%)
  between operations  14.5 us (2%)
    psum x1, waiting for transfers between devices, shards(): grad_short = lax.psum(jnp.stack(partial_short), ('ctx', 'dp'))  425 us
    all_to_all x1, waiting for transfers between devices, shards(): lax.all_to_all(back_rows, 'ctx', split_axis=0, concat_axis=1, tiled=True)  27.9 us
    all_to_all x1, waiting for transfers between devices, shards(): lax.all_to_all(d_conv, 'ctx', split_axis=1, concat_axis=0, tiled=True)  27.1 us
    reduce_sum x8, other arithmetic, one_mode(): grad_row = jnp.sum(forward * cot_f, axis=(1, 2))  25.3 us
    all_to_all x1, waiting for transfers between devices, shards(): lax.all_to_all(gated, 'ctx', split_axis=1, concat_axis=0, tiled=True)  24.2 us
    all_to_all x1, starting transfers between devices, shards(): lax.all_to_all(gated, 'ctx', split_axis=1, concat_axis=0, tiled=True)  18.3 us
    unnamed x46, local copies, waits for them, and re-layouts  15 us
    psum x1, blocking collectives, shards(): grad_residue = lax.psum(partial_value, 'dp')  14.6 us
  transfers between devices with their start and end apart: 7, of which 6 were waited for; matrix products, arithmetic and copies ran while one was open for 5% of the time, Pallas kernels for 0%

commit v1 on v0

v1 whole, which is shorter than its diff:
```python
import functools

import jax
import jax.numpy as jnp
from jax import lax
from jax.experimental import pallas as pl
from jax.experimental.pallas import tpu as pltpu
from jax.sharding import PartitionSpec as P

MESH = pl.DeviceIdType.MESH
ROWS = 128
CHANNELS = 2048
MODES = 8
LANES = 128
BLOCKS = CHANNELS // LANES
WIDE = 256
NZ = 16
NY = 4
NDP = 8
PLANE = NY * NDP
QUARTER = CHANNELS // NY
F32 = jnp.float32
BF16 = jnp.bfloat16


def split_bf16(value):
    high = value.astype(BF16).astype(F32)
    return high, value - high


def two_row_tile(first, second, at):
    width = first.shape[1]
    row = lax.broadcasted_iota(jnp.int32, (8, width), 0)
    return jnp.where(row == at, first, jnp.where(row == at + 1, second, 0.0))


def rate_rows(rate_ref, width):
    row = lax.broadcasted_iota(jnp.int32, (MODES, width), 0)
    total = jnp.zeros((MODES, width), F32)
    for mode in range(MODES):
        total = jnp.where(row == mode, rate_ref[mode], total)
    return total


def plane_peer(index):
    return index // NDP, lax.rem(index, NDP)


def operator_kernel(
    rate_ref,
    q_ref,
    k_ref,
    v_ref,
    go_ref,
    before_ref,
    after_ref,
    filter_ref,
    residue_ref,
    mixed_ref,
    gq_ref,
    gk_ref,
    gv_ref,
    gres_ref,
    gshort_ref,
    short_q,
    short_k,
    short_v,
    gated,
    d_conv,
    tail_gd,
    fwd_table,
    bwd_table,
    modal,
    conv_local,
    back_local,
    res_local,
    ends,
    y_send,
    y_recv,
    z_send,
    z_recv,
    b_send,
    b_recv,
    enter,
    edge,
    r_send,
    r_recv,
    p_send,
    p_recv,
    a_recv,
    turned,
    send_sems,
    recv_sems,
):
    ctx = lax.axis_index("ctx")
    dp = lax.axis_index("dp")
    z = ctx // NY
    y = lax.rem(ctx, NY)
    plane = y * NDP + dp

    barrier = pltpu.get_barrier_semaphore()

    def greet_line(step, carry):
        peer = lax.rem(z + step, NZ)
        pl.semaphore_signal(
            barrier, inc=1, device_id={"ctx": peer * NY + y}, device_id_type=MESH
        )
        return carry

    def greet_plane(step, carry):
        peer_y, peer_dp = plane_peer(lax.rem(plane + step, PLANE))
        pl.semaphore_signal(
            barrier,
            inc=1,
            device_id={"ctx": z * NY + peer_y, "dp": peer_dp},
            device_id_type=MESH,
        )
        return carry

    lax.fori_loop(1, NZ, greet_line, 0)
    lax.fori_loop(1, PLANE, greet_plane, 0)

    def taps(branch, lanes):
        return [filter_ref[branch, j : j + 1, lanes] for j in range(3)]

    def before_tile(branch, lanes):
        rows = before_ref[branch, :, lanes].astype(F32)
        return two_row_tile(rows[0:1], rows[1:2], 6)

    def after_tile(branch, lanes):
        rows = after_ref[branch, :, lanes].astype(F32)
        return two_row_tile(rows[0:1], rows[1:2], 0)

    inputs = (q_ref, k_ref, v_ref)
    shorts = (short_q, short_k, short_v)

    def short_step(block, carry):
        lanes = pl.ds(pl.multiple_of(block * LANES, LANES), LANES)
        results = []
        for branch in range(3):
            values = inputs[branch][:, lanes].astype(F32)
            extended = jnp.concatenate(
                [before_tile(branch, lanes), values, after_tile(branch, lanes)], axis=0
            )
            first, second, third = taps(branch, lanes)
            total = (
                first * extended[8:]
                + second * pltpu.roll(extended, 1, 0)[8:]
                + third * pltpu.roll(extended, 2, 0)[8:]
            )
            shorts[branch][:, lanes] = total
            results.append(total)
        query, keyed, valued = results
        cot = jnp.concatenate([go_ref[:, lanes].astype(F32), after_tile(3, lanes)], axis=0)
        gate = (keyed * valued).astype(BF16)
        d_out = (cot * query).astype(BF16)
        gated[:, lanes] = gate[:ROWS]
        d_conv[:, lanes] = d_out[:ROWS]
        tail_gd[0:8, lanes] = (keyed[ROWS:] * valued[ROWS:]).astype(BF16).astype(F32)
        tail_gd[8:16, lanes] = (cot[ROWS:] * query[ROWS:]).astype(BF16).astype(F32)
        return carry

    lax.fori_loop(0, BLOCKS, short_step, 0)

    rates = rate_rows(rate_ref, ROWS)
    place = lax.broadcasted_iota(jnp.int32, (MODES, ROWS), 1).astype(F32)
    for slot, offsets, operand in ((0, ROWS - 1.0 - place, gated), (1, place, d_conv)):
        high, low = split_bf16(jnp.exp(-rates * offsets))
        table = jnp.concatenate([high, low], axis=0).astype(BF16)
        product = jnp.dot(table, operand[...], preferred_element_type=F32)
        ends[slot * 8 : slot * 8 + 8, :] = product[:8] + product[8:]

    for part in range(NY):
        y_send[part] = ends[:, part * QUARTER : (part + 1) * QUARTER]

    pl.semaphore_wait(barrier, NZ - 1 + PLANE - 1)

    def y_copy(source, target, step, slot):
        peer = lax.rem(y + step, NY)
        return pltpu.make_async_remote_copy(
            src_ref=source.at[peer],
            dst_ref=target.at[y],
            send_sem=send_sems.at[slot],
            recv_sem=recv_sems.at[slot],
            device_id={"ctx": z * NY + peer},
            device_id_type=MESH,
        )

    def settle(source, target, count, slot):
        done = pltpu.make_async_remote_copy(
            src_ref=source.at[pl.ds(0, count)],
            dst_ref=target.at[pl.ds(0, count)],
            send_sem=send_sems.at[slot],
            recv_sem=recv_sems.at[slot],
            device_id={"ctx": z * NY + lax.rem(y + 1, NY)},
            device_id_type=MESH,
        )
        done.wait_send()
        done.wait_recv()

    for step in range(1, NY):
        y_copy(y_send, y_recv, step, 0).start()
    y_recv[y] = y_send[y]

    row_at = lax.broadcasted_iota(jnp.int32, (ROWS, ROWS), 0)
    col_at = lax.broadcasted_iota(jnp.int32, (ROWS, ROWS), 1)
    for mode in range(MODES):
        speed = rate_ref[mode]
        here = slice(mode * ROWS, (mode + 1) * ROWS)
        for table, lag in ((fwd_table, row_at - col_at), (bwd_table, col_at - row_at)):
            power = jnp.exp(-speed * jnp.maximum(lag, 0).astype(F32))
            high, low = split_bf16(jnp.where(lag >= 0, power, 0.0))
            table[here, 0:ROWS] = high.astype(BF16)
            table[here, ROWS : 2 * ROWS] = low.astype(BF16)

    settle(y_send, y_recv, NY - 1, 0)

    speeds = rate_rows(rate_ref, QUARTER)
    step_decay = jnp.exp(-speeds * float(ROWS))
    group_decay = jnp.exp(-speeds * float(ROWS * NY))

    def fold(value):
        return jnp.concatenate([value[:, : QUARTER // 2], value[:, QUARTER // 2 :]], axis=0)

    def unfold(value):
        return jnp.concatenate([value[:8], value[8:]], axis=1)

    ahead_total = y_recv[0, 0:8]
    back_total = y_recv[NY - 1, 8:16]
    for index in range(1, NY):
        ahead_total = ahead_total * step_decay + y_recv[index, 0:8]
        back_total = back_total * step_decay + y_recv[NY - 1 - index, 8:16]
    z_send[0] = fold(ahead_total).astype(BF16)
    z_send[1] = fold(back_total).astype(BF16)

    def z_start(step, carry):
        peer = lax.rem(z + step, NZ)
        pltpu.make_async_remote_copy(
            src_ref=z_send.at[jnp.where(peer < z, 1, 0)],
            dst_ref=z_recv.at[z],
            send_sem=send_sems.at[1],
            recv_sem=recv_sems.at[1],
            device_id={"ctx": peer * NY + y},
            device_id_type=MESH,
        ).start()
        return carry

    lax.fori_loop(1, NZ, z_start, 0)
    z_recv[z] = jnp.zeros((16, QUARTER // 2), BF16)

    gain_rows = jnp.sqrt(1.0 - jnp.exp(-2.0 * rate_rows(rate_ref, WIDE)))

    def modal_step(block, carry):
        lanes = pl.ds(pl.multiple_of(block * WIDE, WIDE), WIDE)
        columns = residue_ref[:, lanes] * gain_rows
        source = gated[:, lanes]
        modal[...] = jnp.dot(
            fwd_table[...],
            jnp.concatenate([source, source], axis=0),
            preferred_element_type=F32,
        )
        cot = d_conv[:, lanes].astype(F32)
        total = jnp.zeros((ROWS, WIDE), F32)
        for mode in range(MODES):
            state = modal[mode * ROWS : (mode + 1) * ROWS, :]
            total = total + columns[mode : mode + 1] * state
            res_local[mode : mode + 1, lanes] = jnp.sum(cot * state, axis=0, keepdims=True)
        conv_local[:, lanes] = total
        source = d_conv[:, lanes]
        modal[...] = jnp.dot(
            bwd_table[...],
            jnp.concatenate([source, source], axis=0),
            preferred_element_type=F32,
        )
        total = jnp.zeros((ROWS, WIDE), F32)
        for mode in range(MODES):
            total = total + columns[mode : mode + 1] * modal[mode * ROWS : (mode + 1) * ROWS, :]
        back_local[:, lanes] = total
        return carry

    lax.fori_loop(0, CHANNELS // WIDE, modal_step, 0)

    done = pltpu.make_async_remote_copy(
        src_ref=z_recv.at[pl.ds(0, NZ - 1)],
        dst_ref=z_recv.at[pl.ds(0, NZ - 1)],
        send_sem=send_sems.at[1],
        recv_sem=recv_sems.at[1],
        device_id={"ctx": lax.rem(z + 1, NZ) * NY + y},
        device_id_type=MESH,
    )
    done.wait_send()
    done.wait_recv()

    start = jnp.zeros((MODES, QUARTER), F32)
    finish = jnp.zeros((MODES, QUARTER), F32)
    for index in range(NZ):
        start = jnp.where(
            index < z, start * group_decay + unfold(z_recv[index].astype(F32)), start
        )
        other = NZ - 1 - index
        finish = jnp.where(
            other > z, finish * group_decay + unfold(z_recv[other].astype(F32)), finish
        )
    for index in range(NY):
        b_send[index, 0:8] = start
        start = start * step_decay + y_recv[index, 0:8]
        other = NY - 1 - index
        b_send[other, 8:16] = finish
        finish = finish * step_decay + y_recv[other, 8:16]

    for step in range(1, NY):
        y_copy(b_send, b_recv, step, 2).start()
    b_recv[y] = b_send[y]
    settle(b_send, b_recv, NY - 1, 2)

    wide_speeds = rate_rows(rate_ref, QUARTER)
    one = jnp.exp(-wide_speeds)
    gains = jnp.sqrt(1.0 - jnp.exp(-2.0 * wide_speeds))
    for part in range(NY):
        lanes = slice(part * QUARTER, (part + 1) * QUARTER)
        columns = residue_ref[:, lanes] * gains
        state = b_recv[part, 0:8]
        costate = b_recv[part, 8:16]
        for slot, value in ((0, columns * state), (1, columns * costate)):
            high, low = split_bf16(value)
            enter[slot, :, lanes] = jnp.concatenate([high, low, high, low], axis=0).astype(BF16)
        out_state = state * step_decay + ends[0:8, lanes]
        next_first = one * out_state + tail_gd[0:1, lanes]
        next_second = one * next_first + tail_gd[1:2, lanes]
        back_second = (costate - tail_gd[8:9, lanes]) / one
        edge[0:8, lanes] = two_row_tile(
            jnp.sum(columns * next_first, axis=0, keepdims=True),
            jnp.sum(columns * next_second, axis=0, keepdims=True),
            0,
        )
        edge[8:16, lanes] = two_row_tile(
            jnp.sum(columns * costate, axis=0, keepdims=True),
            jnp.sum(columns * back_second, axis=0, keepdims=True),
            0,
        )
        total = gains * (res_local[:, lanes] + state * one * ends[8:16, lanes])
        for offset in range(QUARTER // LANES):
            block = part * (QUARTER // LANES) + offset
            r_send[2 * block + 1, 0:8] = total[:, offset * LANES : (offset + 1) * LANES]
            r_send[2 * block + 1, 8:9] = jnp.zeros((1, LANES), F32)

    lane_at = lax.broadcasted_iota(jnp.int32, (ROWS, 4 * MODES), 1)
    lane_rate = jnp.zeros((ROWS, 4 * MODES), F32)
    for mode in range(MODES):
        lane_rate = jnp.where(lax.rem(lane_at, MODES) == mode, rate_ref[mode], lane_rate)
    place = lax.broadcasted_iota(jnp.int32, (ROWS, 4 * MODES), 0).astype(F32)

    def spread(offsets):
        high, low = split_bf16(jnp.exp(-lane_rate * offsets))
        return jnp.where(lane_at < 2 * MODES, high, low).astype(BF16)

    spread_fwd = spread(place + 1.0)
    spread_back = spread(ROWS - place)
    outs = (gq_ref, gk_ref, gv_ref)

    def final_step(block, carry):
        lanes = pl.ds(pl.multiple_of(block * LANES, LANES), LANES)
        conv = conv_local[:, lanes] + jnp.dot(
            spread_fwd, enter[0, :, lanes], preferred_element_type=F32
        )
        back = back_local[:, lanes] + jnp.dot(
            spread_back, enter[1, :, lanes], preferred_element_type=F32
        )
        conv_ext = jnp.concatenate([conv, edge[0:8, lanes]], axis=0)
        back_ext = jnp.concatenate([back, edge[8:16, lanes]], axis=0)
        cot = jnp.concatenate([go_ref[:, lanes].astype(F32), after_tile(3, lanes)], axis=0)
        mixed_ref[:, lanes] = (short_q[0:ROWS, lanes] * conv).astype(BF16)
        d_shorts = (cot * conv_ext, back_ext * short_v[:, lanes], back_ext * short_k[:, lanes])
        for branch in range(3):
            value = d_shorts[branch]
            first, second, third = taps(branch, lanes)
            total = (
                first * value[:ROWS]
                + second * pltpu.roll(value, ROWS + 8 - 1, 0)[:ROWS]
                + third * pltpu.roll(value, ROWS + 8 - 2, 0)[:ROWS]
            )
            outs[branch][:, lanes] = total.astype(BF16)
            extended = jnp.concatenate(
                [before_tile(branch, lanes), inputs[branch][:, lanes].astype(F32)], axis=0
            )
            for tap_at in range(3):
                moved = pltpu.roll(extended, tap_at, 0)[8:] if tap_at else extended[8:]
                at = branch * 3 + tap_at
                r_send[2 * block, at : at + 1] = jnp.sum(
                    value[:ROWS] * moved, axis=0, keepdims=True
                )
        return carry

    lax.fori_loop(0, BLOCKS, final_step, 0)

    def plane_start(source_of, target, slot):
        def start_one(step, carry):
            peer = lax.rem(plane + step, PLANE)
            peer_y, peer_dp = plane_peer(peer)
            pltpu.make_async_remote_copy(
                src_ref=source_of(peer),
                dst_ref=target.at[plane],
                send_sem=send_sems.at[slot],
                recv_sem=recv_sems.at[slot],
                device_id={"ctx": z * NY + peer_y, "dp": peer_dp},
                device_id_type=MESH,
            ).start()
            return carry

        lax.fori_loop(1, PLANE, start_one, 0)

    plane_start(lambda peer: r_send.at[peer], r_recv, 3)
    r_recv[plane] = r_send[plane]
    settle(r_send, r_recv, PLANE - 1, 3)
    total = r_recv[0]
    for index in range(1, PLANE):
        total = total + r_recv[index]
    p_send[...] = total

    def line_start(step, carry):
        peer = lax.rem(z + step, NZ)
        pltpu.make_async_remote_copy(
            src_ref=p_send,
            dst_ref=p_recv.at[z],
            send_sem=send_sems.at[4],
            recv_sem=recv_sems.at[4],
            device_id={"ctx": peer * NY + y},
            device_id_type=MESH,
        ).start()
        return carry

    lax.fori_loop(1, NZ, line_start, 0)
    p_recv[z] = p_send[...]
    settle(p_recv, p_recv, NZ - 1, 4)
    total = p_recv[0]
    for index in range(1, NZ):
        total = total + p_recv[index]
    a_recv[plane] = total
    plane_start(lambda peer: a_recv.at[plane], a_recv, 5)
    settle(a_recv, a_recv, PLANE - 1, 5)
    for block in range(BLOCKS):
        gshort_ref[:, block * LANES : (block + 1) * LANES] = a_recv[2 * block]
    mine = a_recv[2 * z + 1][0:8]
    turned[...] = mine.T
    gres_ref[...] = turned[pl.ds(pl.multiple_of(y * 32, 32), 32), :]


def shards(q_in, k_in, v_in, grad_out, short_filter, residue, rate):
    inputs = (q_in[0], k_in[0], v_in[0], grad_out[0])
    count = lax.axis_size("ctx")
    tails = jnp.stack([item[ROWS - 2 :] for item in inputs[:3]])
    heads = jnp.stack([item[:2] for item in inputs])
    before = lax.ppermute(tails, "ctx", [(i, i + 1) for i in range(count - 1)])
    after = lax.ppermute(heads, "ctx", [(i + 1, i) for i in range(count - 1)])
    vmem = pl.BlockSpec(memory_space=pltpu.VMEM)
    smem = pl.BlockSpec(memory_space=pltpu.SMEM)
    block = jax.ShapeDtypeStruct((ROWS, CHANNELS), BF16)
    mixed, gq, gk, gv, gres, gshort = pl.pallas_call(
        operator_kernel,
        out_shape=(
            block,
            block,
            block,
            block,
            jax.ShapeDtypeStruct((CHANNELS // 64, MODES), F32),
            jax.ShapeDtypeStruct((9, CHANNELS), F32),
        ),
        in_specs=[smem] + [vmem] * 8,
        out_specs=(vmem,) * 6,
        scratch_shapes=[
            pltpu.VMEM((ROWS + 8, CHANNELS), F32),
            pltpu.VMEM((ROWS + 8, CHANNELS), F32),
            pltpu.VMEM((ROWS + 8, CHANNELS), F32),
            pltpu.VMEM((ROWS, CHANNELS), BF16),
            pltpu.VMEM((ROWS, CHANNELS), BF16),
            pltpu.VMEM((16, CHANNELS), F32),
            pltpu.VMEM((MODES * ROWS, 2 * ROWS), BF16),
            pltpu.VMEM((MODES * ROWS, 2 * ROWS), BF16),
            pltpu.VMEM((MODES * ROWS, WIDE), F32),
            pltpu.VMEM((ROWS, CHANNELS), F32),
            pltpu.VMEM((ROWS, CHANNELS), F32),
            pltpu.VMEM((MODES, CHANNELS), F32),
            pltpu.VMEM((16, CHANNELS), F32),
            pltpu.VMEM((NY, 16, QUARTER), F32),
            pltpu.VMEM((NY, 16, QUARTER), F32),
            pltpu.VMEM((2, 16, QUARTER // 2), BF16),
            pltpu.VMEM((NZ, 16, QUARTER // 2), BF16),
            pltpu.VMEM((NY, 16, QUARTER), F32),
            pltpu.VMEM((NY, 16, QUARTER), F32),
            pltpu.VMEM((2, 4 * MODES, CHANNELS), BF16),
            pltpu.VMEM((16, CHANNELS), F32),
            pltpu.VMEM((PLANE, 9, LANES), F32),
            pltpu.VMEM((PLANE, 9, LANES), F32),
            pltpu.VMEM((9, LANES), F32),
            pltpu.VMEM((NZ, 9, LANES), F32),
            pltpu.VMEM((PLANE, 9, LANES), F32),
            pltpu.VMEM((LANES, MODES), F32),
            pltpu.SemaphoreType.DMA((6,)),
            pltpu.SemaphoreType.DMA((6,)),
        ],
        name="operator",
        compiler_params=pltpu.CompilerParams(
            collective_id=0, has_side_effects=True, vmem_limit_bytes=48 << 20
        ),
    )(rate, *inputs, before, after, short_filter, residue.T)
    return (
        mixed[None],
        gq[None],
        gk[None],
        gv[None],
        gres,
        gshort.reshape(3, 3, CHANNELS),
    )


def solution(mesh):
    placed = P("dp", "ctx", None)
    return jax.shard_map(
        shards,
        mesh=mesh,
        in_specs=(placed, placed, placed, placed, P(), P(), P()),
        out_specs=(placed, placed, placed, placed, P("ctx", None), P()),
        check_vma=False,
    )
```

time: 705 us -> 84.6 us (0.12)
  waiting for transfers between devices: 508 us -> 0.93 us
  Pallas kernels: 0 us -> 64.6 us
  other arithmetic: 54 us -> 0.1 us
  starting transfers between devices: 50.4 us -> 5.95 us
  local copies, waits for them, and re-layouts: 39.1 us -> 11.8 us
  matrix products: 16.5 us -> 0 us
  blocking collectives: 14.6 us -> 0 us
  between operations: 14.5 us -> 0.7 us
    psum x1 -> x0, waiting for transfers between devices: 425 us -> none  [shards(): grad_short = lax.psum(jnp.stack(partial_short), ('ctx', 'dp'))]
    all_to_all x4 -> x0, waiting for transfers between devices: 82 us -> none  [the longest x1 27.9 us: shards(): lax.all_to_all(back_rows, 'ctx', split_axis=0, concat_axis=1, tiled=True)]
    pallas_call x0 -> x1, Pallas kernels: none -> 64.6 us  [shards(): pl.pallas_call(operator_kernel, out_shape=(block, block, block, block, ja...]
    all_to_all x4 -> x0, starting transfers between devices: 45.1 us -> none  [the longest x1 18.3 us: shards(): lax.all_to_all(gated, 'ctx', split_axis=1, concat_axis=0, tiled=True)]
    reduce_sum x10 -> x0, other arithmetic: 34.6 us -> none  [the longest x8 25.3 us: one_mode(): grad_row = jnp.sum(forward * cot_f, axis=(1, 2))]
    dot_general x32 -> x0, matrix products: 16.5 us -> none  [the longest x8 11.2 us: one_mode(): jnp.einsum('ts,cnt->cns', kernel, cotangent, preferred_element_type=jnp.f...]
    psum x1 -> x0, blocking collectives: 14.6 us -> none  [shards(): grad_residue = lax.psum(partial_value, 'dp')]
    convert_element_type x8 -> x0, other arithmetic: 10.9 us -> none  [the longest x1 4.51 us: shards(): gated = (keyed * valued).astype(jnp.bfloat16)]
  transfers between devices with their start and end apart: 7 -> 2, of which waited for: 6 -> 1; matrix products, arithmetic and copies ran while one was open for 5% -> 0% of each run, Pallas kernels for 0% -> 0%
where the time goes in v1:
time: 84.6 us; the launch traced here: 84.1 us
  Pallas kernels  64.6 us (76%)
  local copies, waits for them, and re-layouts  11.8 us (14%)
  starting transfers between devices  5.95 us (7%)
  waiting for transfers between devices  0.93 us (1%)
    pallas_call x1, Pallas kernels, shards(): pl.pallas_call(operator_kernel, out_shape=(block, block, block, block, ja...  64.6 us
    unnamed x19, local copies, waits for them, and re-layouts  8.66 us
    ppermute x1, starting transfers between devices, shards(): before = lax.ppermute(tails, 'ctx', [(i, i + 1) for i in range(count - 1)])  4.66 us
    slice x3, local copies, waits for them, and re-layouts, shards(): heads = jnp.stack([item[:2] for item in inputs])  2.43 us
  transfers between devices with their start and end apart: 2, of which 1 were waited for; matrix products, arithmetic and copies ran while one was open for 0% of the time, Pallas kernels for 0%

profile of v1, /device:TPU:1, one launch (start us, length us, event | category | flops | bytes accessed | tf_op | source)
XLA Modules:
  0.0 84.1 jit_solution(15579473511761425300)
XLA Ops:
  0.6 0.8 slice.34
  1.4 0.8 fusion.2
  2.2 0.0 copy-start.4
  2.2 0.9 %fusion = (bf16[1,2,2048]{2,1,0:T(2,128)(2,1)S(1)}, bf16[1,2,2048]{2,1,0:T(2,128)(2,1)S(1)}, bf16[1,2,2048]{2,1,0:T(2,128)(2,1)S(1)}, bf16[1,2,2048]{2,1,0:T(2,128)(2,1)S(1)}) fusion(bf16[1,128,2048]{2,1,0:T(8,128)(2,1)} %param.7, bf16[1,128,2048]{2,1,0:T(8,128)(2,1)} %param.8), kind=kLoop, calls=%fused_computation.2 | loop fusion | bytes 65536 | tf_op jit(solution)/shard_map/slice | solution.py:452
  3.1 0.0 copy-start.5
  3.1 0.1 pad_maximum_fusion
  3.2 1.3 %collective-permute-start.1 = (bf16[4,2,2048]{2,1,0:T(2,128)(2,1)S(1)}, bf16[4,2,2048]{2,1,0:T(2,128)(2,1)S(1)}, u32[]{:S(2)}, u32[]{:S(2)}) collective-permute-start(bf16[4,2,2048]{2,1,0:T(2,128)(2,1)S(1)} %pad_maximum_fusion), channel_id=1, source_target_pairs={{8,0},{16,8},{24,16},{32,24},{40,32},{48,40},{56,48},{64,56},{72,6... | collective-permute-start | bytes 98312 | tf_op jit(solution)/shard_map/ppermute | solution.py:454
  4.5 4.7 %collective-permute-start = (bf16[3,2,2048]{2,1,0:T(2,128)(2,1)S(1)}, bf16[3,2,2048]{2,1,0:T(2,128)(2,1)S(1)}, u32[]{:S(2)}, u32[]{:S(2)}) collective-permute-start(bf16[3,2,2048]{2,1,0:T(2,128)(2,1)S(1)} %pad_maximum_fusion.1), channel_id=1, source_target_pairs={{0,8},{8,16},{16,24},{24,32},{32,40},{40,48},{48,56},{56,64},{64,7... | collective-permute-start | bytes 73736 | tf_op jit(solution)/shard_map/ppermute | solution.py:453
  9.2 0.9 %collective-permute-done.before_ref = bf16[3,2,2048]{2,1,0:T(2,128)(2,1)S(1)} collective-permute-done((bf16[3,2,2048]{2,1,0:T(2,128)(2,1)S(1)}, bf16[3,2,2048]{2,1,0:T(2,128)(2,1)S(1)}, u32[]{:S(2)}, u32[]{:S(2)}) %collective-permute-start) | collective-permute-done | bytes 24608 | tf_op jit(solution)/shard_map/ppermute | solution.py:453
  10.1 0.0 collective-permute-done.1.after_ref
  10.1 0.0 copy-start.6
  10.1 0.0 copy-done.4
  10.1 0.0 copy-done.5
  10.1 0.6 copy-done.6
  10.8 0.0 copy-start
  10.8 1.0 %copy-done = bf16[1,128,2048]{2,1,0:T(8,128)(2,1)S(1)} copy-done((bf16[1,128,2048]{2,1,0:T(8,128)(2,1)S(1)}, bf16[1,128,2048]{2,1,0:T(8,128)(2,1)}, u32[]{:S(2)}) %copy-start) | copy-done | bytes 524312
  11.8 0.0 copy-start.1
  11.8 1.0 %copy-done.1 = bf16[1,128,2048]{2,1,0:T(8,128)(2,1)S(1)} copy-done((bf16[1,128,2048]{2,1,0:T(8,128)(2,1)S(1)}, bf16[1,128,2048]{2,1,0:T(8,128)(2,1)}, u32[]{:S(2)}) %copy-start.1) | copy-done | bytes 524312
  12.8 0.0 copy-start.2
  12.8 1.0 %copy-done.2 = bf16[1,128,2048]{2,1,0:T(8,128)(2,1)S(1)} copy-done((bf16[1,128,2048]{2,1,0:T(8,128)(2,1)S(1)}, bf16[1,128,2048]{2,1,0:T(8,128)(2,1)}, u32[]{:S(2)}) %copy-start.2) | copy-done | bytes 524312
  13.9 0.0 copy-start.3
  13.9 1.0 %copy-done.3 = bf16[1,128,2048]{2,1,0:T(8,128)(2,1)S(1)} copy-done((bf16[1,128,2048]{2,1,0:T(8,128)(2,1)S(1)}, bf16[1,128,2048]{2,1,0:T(8,128)(2,1)}, u32[]{:S(2)}) %copy-start.3) | copy-done | bytes 524312
  14.9 64.6 %operator.1 = (bf16[128,2048]{1,0:T(8,128)(2,1)S(1)}, bf16[128,2048]{1,0:T(8,128)(2,1)S(1)}, bf16[128,2048]{1,0:T(8,128)(2,1)S(1)}, bf16[128,2048]{1,0:T(8,128)(...) custom-call(f32[8]{0:T(128)S(1)} %copy-done.6, bf16[128,2048]{1,0:T(8,128)(2,1)S(1)} %bitcast.9, ...), custom_call_target="tpu_custom_call" | custom-call | tf_op jit(solution)/shard_map/operator/pallas_call | solution.py:458
  79.6 0.7 copy.13
  80.2 0.7 reshape.29
  80.9 0.8 copy.18
  81.7 0.8 copy.19
  82.5 0.8 copy.20
  83.3 0.8 copy.21
  (1 shorter events, 0.0 us)
Async XLA Ops:
  2.2 7.9 %copy-start.4 = (f32[3,3,2048]{2,1,0:T(4,128)S(1)}, f32[3,3,2048]{2,1,0:T(4,128)}, u32[]{:S(2)}) copy-start(f32[3,3,2048]{2,1,0:T(4,128)} %filter_ref.1) | copy-start | bytes 221188
  3.1 7.0 %copy-start.5 = (f32[2048,8]{0,1:T(8,128)S(1)}, f32[2048,8]{0,1:T(8,128)}, u32[]{:S(2)}) copy-start(f32[2048,8]{0,1:T(8,128)} %param.12) | copy-start | bytes 196612
  3.2 6.9 %collective-permute-start.1 = (bf16[4,2,2048]{2,1,0:T(2,128)(2,1)S(1)}, bf16[4,2,2048]{2,1,0:T(2,128)(2,1)S(1)}, u32[]{:S(2)}, u32[]{:S(2)}) collective-permute-start(bf16[4,2,2048]{2,1,0:T(2,128)(2,1)S(1)} %pad_maximum_fusion), channel_id=1, source_target_pairs={{8,0},{16,8},{24,16},{32,24},{40,32},{48,40},{56,48},{64,56},{72,6... | collective-permute-start | bytes 98312 | tf_op jit(solution)/shard_map/ppermute | solution.py:454
  4.5 5.6 %collective-permute-start = (bf16[3,2,2048]{2,1,0:T(2,128)(2,1)S(1)}, bf16[3,2,2048]{2,1,0:T(2,128)(2,1)S(1)}, u32[]{:S(2)}, u32[]{:S(2)}) collective-permute-start(bf16[3,2,2048]{2,1,0:T(2,128)(2,1)S(1)} %pad_maximum_fusion.1), channel_id=1, source_target_pairs={{0,8},{8,16},{16,24},{24,32},{32,40},{40,48},{48,56},{56,64},{64,7... | collective-permute-start | bytes 73736 | tf_op jit(solution)/shard_map/ppermute | solution.py:453
  10.1 0.7 copy-start.6
  10.8 1.0 %copy-start = (bf16[1,128,2048]{2,1,0:T(8,128)(2,1)S(1)}, bf16[1,128,2048]{2,1,0:T(8,128)(2,1)}, u32[]{:S(2)}) copy-start(bf16[1,128,2048]{2,1,0:T(8,128)(2,1)} %param.7) | copy-start | bytes 1572868
  11.8 1.0 %copy-start.1 = (bf16[1,128,2048]{2,1,0:T(8,128)(2,1)S(1)}, bf16[1,128,2048]{2,1,0:T(8,128)(2,1)}, u32[]{:S(2)}) copy-start(bf16[1,128,2048]{2,1,0:T(8,128)(2,1)} %param.8) | copy-start | bytes 1572868
  12.8 1.0 %copy-start.2 = (bf16[1,128,2048]{2,1,0:T(8,128)(2,1)S(1)}, bf16[1,128,2048]{2,1,0:T(8,128)(2,1)}, u32[]{:S(2)}) copy-start(bf16[1,128,2048]{2,1,0:T(8,128)(2,1)} %param.9) | copy-start | bytes 1572868
  13.9 1.0 %copy-start.3 = (bf16[1,128,2048]{2,1,0:T(8,128)(2,1)S(1)}, bf16[1,128,2048]{2,1,0:T(8,128)(2,1)}, u32[]{:S(2)}) copy-start(bf16[1,128,2048]{2,1,0:T(8,128)(2,1)} %param.10) | copy-start | bytes 1572868

commit v2 on v1

v2 whole, which is shorter than its diff:
```python
import functools

import jax
import jax.numpy as jnp
from jax import lax
from jax.experimental import pallas as pl
from jax.experimental.pallas import tpu as pltpu
from jax.sharding import PartitionSpec as P

MESH = pl.DeviceIdType.MESH
ROWS = 128
CHANNELS = 2048
MODES = 8
LANES = 128
BLOCKS = CHANNELS // LANES
WIDE = 256
NZ = 16
NY = 4
NDP = 8
PLANE = NY * NDP
QUARTER = CHANNELS // NY
GRANT = 56 << 20
F32 = jnp.float32
BF16 = jnp.bfloat16


def split_bf16(value):
    high = value.astype(BF16).astype(F32)
    return high, value - high


def two_row_tile(first, second, at):
    width = first.shape[1]
    row = lax.broadcasted_iota(jnp.int32, (8, width), 0)
    return jnp.where(row == at, first, jnp.where(row == at + 1, second, 0.0))


def rate_rows(rate_ref, width):
    row = lax.broadcasted_iota(jnp.int32, (MODES, width), 0)
    total = jnp.zeros((MODES, width), F32)
    for mode in range(MODES):
        total = jnp.where(row == mode, rate_ref[mode], total)
    return total


def plane_peer(index):
    return index // NDP, lax.rem(index, NDP)


def operator_kernel(
    rate_ref,
    q_hbm,
    k_hbm,
    v_hbm,
    go_hbm,
    filter_ref,
    residue_ref,
    mixed_hbm,
    gq_hbm,
    gk_hbm,
    gv_hbm,
    gres_ref,
    gshort_ref,
    mixed_ref,
    gq_ref,
    gk_ref,
    gv_ref,
    q_ref,
    k_ref,
    v_ref,
    go_ref,
    tail_send,
    head_send,
    tail_recv,
    head_recv,
    short_q,
    short_k,
    short_v,
    gated,
    d_conv,
    tail_gd,
    fwd_table,
    bwd_table,
    modal,
    conv_local,
    back_local,
    res_local,
    ends,
    y_send,
    y_recv,
    z_send,
    z_recv,
    b_send,
    b_recv,
    enter,
    edge,
    m_send,
    m_recv,
    l_send,
    l_recv,
    r_send,
    r_recv,
    p_send,
    p_recv,
    short_sum,
    res_sum,
    load_sems,
    store_sems,
    send_sems,
    recv_sems,
):
    ctx = lax.axis_index("ctx")
    dp = lax.axis_index("dp")
    z = ctx // NY
    y = lax.rem(ctx, NY)
    plane = y * NDP + dp

    inputs = (q_ref, k_ref, v_ref, go_ref)
    loads = [
        pltpu.make_async_copy(source, target, load_sems.at[index])
        for index, (source, target) in enumerate(zip((q_hbm, k_hbm, v_hbm, go_hbm), inputs))
    ]
    for load in loads:
        load.start()

    barrier = pltpu.get_barrier_semaphore()
    count = NZ * NY
    following = lax.rem(ctx + 1, count)
    preceding = lax.rem(ctx + count - 1, count)
    for neighbour in (following, preceding):
        pl.semaphore_signal(
            barrier, inc=1, device_id={"ctx": neighbour}, device_id_type=MESH
        )

    def greet_line(step, carry):
        peer = lax.rem(z + step, NZ)
        pl.semaphore_signal(
            barrier, inc=1, device_id={"ctx": peer * NY + y}, device_id_type=MESH
        )
        return carry

    def greet_plane(step, carry):
        peer_y, peer_dp = plane_peer(lax.rem(plane + step, PLANE))
        pl.semaphore_signal(
            barrier,
            inc=1,
            device_id={"ctx": z * NY + peer_y, "dp": peer_dp},
            device_id_type=MESH,
        )
        return carry

    lax.fori_loop(1, NZ, greet_line, 0)
    lax.fori_loop(1, PLANE, greet_plane, 0)

    def taps(branch, lanes):
        return [filter_ref[branch, j : j + 1, lanes] for j in range(3)]

    for load in loads:
        load.wait()

    row_eight = lax.broadcasted_iota(jnp.int32, (8, CHANNELS), 0)
    tails = jnp.zeros((8, CHANNELS), F32)
    heads = jnp.zeros((8, CHANNELS), F32)
    for branch in range(4):
        last = inputs[branch][ROWS - 16 : ROWS, :].astype(F32)
        first = inputs[branch][0:16, :].astype(F32)
        for index in range(2):
            here = row_eight == 2 * branch + index
            heads = jnp.where(here, first[index : index + 1], heads)
            if branch < 3:
                tails = jnp.where(here, last[14 + index : 15 + index], tails)
    tail_send[...] = tails.astype(BF16)
    head_send[...] = heads.astype(BF16)

    pl.semaphore_wait(barrier, NZ - 1 + PLANE - 1 + 2)
    halos = [
        pltpu.make_async_remote_copy(
            src_ref=source,
            dst_ref=target,
            send_sem=send_sems.at[slot],
            recv_sem=recv_sems.at[slot],
            device_id={"ctx": neighbour},
            device_id_type=MESH,
        )
        for slot, source, target, neighbour in (
            (6, tail_send, tail_recv, following),
            (7, head_send, head_recv, preceding),
        )
    ]
    for halo in halos:
        halo.start()

    def before_tile(branch, lanes):
        rows = tail_recv[:, lanes].astype(F32)[2 * branch : 2 * branch + 2]
        tile = two_row_tile(rows[0:1], rows[1:2], 6)
        return jnp.where(ctx == 0, 0.0, tile)

    def after_tile(branch, lanes):
        rows = head_recv[:, lanes].astype(F32)[2 * branch : 2 * branch + 2]
        tile = two_row_tile(rows[0:1], rows[1:2], 0)
        return jnp.where(ctx == count - 1, 0.0, tile)

    shorts = (short_q, short_k, short_v)

    def convolve(branch, lanes, extended):
        first, second, third = taps(branch, lanes)
        return (
            first * extended[8:]
            + second * pltpu.roll(extended, 1, 0)[8:]
            + third * pltpu.roll(extended, 2, 0)[8:]
        )

    def short_step(block, carry):
        lanes = pl.ds(pl.multiple_of(block * LANES, LANES), LANES)
        results = []
        for branch in range(3):
            values = inputs[branch][:, lanes].astype(F32)
            extended = jnp.concatenate([jnp.zeros((8, LANES), F32), values], axis=0)
            total = convolve(branch, lanes, extended)
            shorts[branch][0:ROWS, lanes] = total
            results.append(total)
        query, keyed, valued = results
        gated[:, lanes] = (keyed * valued).astype(BF16)
        d_conv[:, lanes] = (go_ref[:, lanes].astype(F32) * query).astype(BF16)
        return carry

    lax.fori_loop(0, BLOCKS, short_step, 0)

    for halo in halos:
        halo.wait_recv()

    def patch_step(block, carry):
        lanes = pl.ds(pl.multiple_of(block * LANES, LANES), LANES)
        firsts = []
        nexts = []
        for branch in range(3):
            values = inputs[branch][0:16, lanes].astype(F32)
            extended = jnp.concatenate([before_tile(branch, lanes), values], axis=0)
            firsts.append(convolve(branch, lanes, extended))
            shorts[branch][0:16, lanes] = firsts[branch]
            values = inputs[branch][ROWS - 16 : ROWS, lanes].astype(F32)[8:]
            extended = jnp.concatenate([values, after_tile(branch, lanes)], axis=0)
            nexts.append(convolve(branch, lanes, extended))
            shorts[branch][ROWS : ROWS + 8, lanes] = nexts[branch]
        gated[0:16, lanes] = (firsts[1] * firsts[2]).astype(BF16)
        d_conv[0:16, lanes] = (go_ref[0:16, lanes].astype(F32) * firsts[0]).astype(BF16)
        tail_gd[0:8, lanes] = (nexts[1] * nexts[2]).astype(BF16).astype(F32)
        tail_gd[8:16, lanes] = (after_tile(3, lanes) * nexts[0]).astype(BF16).astype(F32)
        return carry

    lax.fori_loop(0, BLOCKS, patch_step, 0)

    rates = rate_rows(rate_ref, ROWS)
    place = lax.broadcasted_iota(jnp.int32, (MODES, ROWS), 1).astype(F32)
    for slot, offsets, operand in ((0, ROWS - 1.0 - place, gated), (1, place, d_conv)):
        high, low = split_bf16(jnp.exp(-rates * offsets))
        table = jnp.concatenate([high, low], axis=0).astype(BF16)
        product = jnp.dot(table, operand[...], preferred_element_type=F32)
        ends[slot * 8 : slot * 8 + 8, :] = product[:8] + product[8:]

    for part in range(NY):
        y_send[part] = ends[:, part * QUARTER : (part + 1) * QUARTER]

    def y_copy(source, target, step, slot):
        peer = lax.rem(y + step, NY)
        return pltpu.make_async_remote_copy(
            src_ref=source.at[peer],
            dst_ref=target.at[y],
            send_sem=send_sems.at[slot],
            recv_sem=recv_sems.at[slot],
            device_id={"ctx": z * NY + peer},
            device_id_type=MESH,
        )

    leaving = []

    def settle(target, number, slot):
        done = pltpu.make_async_remote_copy(
            src_ref=target.at[pl.ds(0, number)],
            dst_ref=target.at[pl.ds(0, number)],
            send_sem=send_sems.at[slot],
            recv_sem=recv_sems.at[slot],
            device_id={"ctx": z * NY + lax.rem(y + 1, NY)},
            device_id_type=MESH,
        )
        done.wait_recv()
        leaving.append(done)

    for step in range(1, NY):
        y_copy(y_send, y_recv, step, 0).start()
    y_recv[y] = y_send[y]

    place = lax.broadcasted_iota(jnp.int32, (MODES, ROWS), 1).astype(F32)
    weigh_fwd = jnp.exp(-rates * (place + 1.0)).astype(BF16)
    weigh_back = jnp.exp(-rates * (ROWS - place)).astype(BF16)

    def partner(branch, lanes):
        if branch == 0:
            return go_ref[:, lanes].astype(F32)
        return (short_v if branch == 1 else short_k)[0:ROWS, lanes]

    def moved_rows(branch, lanes):
        extended = jnp.concatenate(
            [before_tile(branch, lanes), inputs[branch][:, lanes].astype(F32)], axis=0
        )
        return [extended[8:]] + [pltpu.roll(extended, tap_at, 0)[8:] for tap_at in (1, 2)]

    def moment_step(block, carry):
        lanes = pl.ds(pl.multiple_of(block * WIDE, WIDE), WIDE)
        part = block // (QUARTER // WIDE)
        inner = pl.ds(pl.multiple_of(lax.rem(block, QUARTER // WIDE) * WIDE, WIDE), WIDE)
        for branch in range(3):
            weigh = weigh_back if branch else weigh_fwd
            other = partner(branch, lanes)
            for tap_at, moved in enumerate(moved_rows(branch, lanes)):
                product = jnp.dot(
                    weigh, (other * moved).astype(BF16), preferred_element_type=F32
                )
                m_send[part, branch * 3 + tap_at, :, inner] = product.astype(BF16)
        return carry

    lax.fori_loop(0, CHANNELS // WIDE, moment_step, 0)

    settle(y_recv, NY - 1, 0)

    speeds = rate_rows(rate_ref, QUARTER)
    step_decay = jnp.exp(-speeds * float(ROWS))
    group_decay = jnp.exp(-speeds * float(ROWS * NY))

    def fold(value):
        return jnp.concatenate([value[:, : QUARTER // 2], value[:, QUARTER // 2 :]], axis=0)

    def unfold(value):
        return jnp.concatenate([value[:8], value[8:]], axis=1)

    ahead_total = y_recv[0, 0:8]
    back_total = y_recv[NY - 1, 8:16]
    for index in range(1, NY):
        ahead_total = ahead_total * step_decay + y_recv[index, 0:8]
        back_total = back_total * step_decay + y_recv[NY - 1 - index, 8:16]
    z_send[0] = fold(ahead_total).astype(BF16)
    z_send[1] = fold(back_total).astype(BF16)

    def z_start(step, carry):
        peer = lax.rem(z + step, NZ)
        pltpu.make_async_remote_copy(
            src_ref=z_send.at[jnp.where(peer < z, 1, 0)],
            dst_ref=z_recv.at[z],
            send_sem=send_sems.at[1],
            recv_sem=recv_sems.at[1],
            device_id={"ctx": peer * NY + y},
            device_id_type=MESH,
        ).start()
        return carry

    lax.fori_loop(1, NZ, z_start, 0)
    z_recv[z] = jnp.zeros((16, QUARTER // 2), BF16)
    for step in range(1, NY):
        y_copy(m_send, m_recv, step, 8).start()
    m_recv[y] = m_send[y]

    row_at = lax.broadcasted_iota(jnp.int32, (ROWS, ROWS), 0)
    col_at = lax.broadcasted_iota(jnp.int32, (ROWS, ROWS), 1)
    for mode in range(MODES):
        speed = rate_ref[mode]
        here = slice(mode * ROWS, (mode + 1) * ROWS)
        for table, lag in ((fwd_table, row_at - col_at), (bwd_table, col_at - row_at)):
            power = jnp.exp(-speed * jnp.maximum(lag, 0).astype(F32))
            high, low = split_bf16(jnp.where(lag >= 0, power, 0.0))
            table[here, 0:ROWS] = high.astype(BF16)
            table[here, ROWS : 2 * ROWS] = low.astype(BF16)

    gain_rows = jnp.sqrt(1.0 - jnp.exp(-2.0 * rate_rows(rate_ref, WIDE)))

    def modal_step(block, carry):
        lanes = pl.ds(pl.multiple_of(block * WIDE, WIDE), WIDE)
        columns = residue_ref[:, lanes] * gain_rows
        source = gated[:, lanes]
        modal[...] = jnp.dot(
            fwd_table[...],
            jnp.concatenate([source, source], axis=0),
            preferred_element_type=F32,
        )
        cot = d_conv[:, lanes].astype(F32)
        total = jnp.zeros((ROWS, WIDE), F32)
        for mode in range(MODES):
            state = modal[mode * ROWS : (mode + 1) * ROWS, :]
            total = total + columns[mode : mode + 1] * state
            res_local[mode : mode + 1, lanes] = jnp.sum(cot * state, axis=0, keepdims=True)
        conv_local[:, lanes] = total
        source = d_conv[:, lanes]
        modal[...] = jnp.dot(
            bwd_table[...],
            jnp.concatenate([source, source], axis=0),
            preferred_element_type=F32,
        )
        total = jnp.zeros((ROWS, WIDE), F32)
        for mode in range(MODES):
            total = total + columns[mode : mode + 1] * modal[mode * ROWS : (mode + 1) * ROWS, :]
        back_local[:, lanes] = total
        return carry

    lax.fori_loop(0, CHANNELS // WIDE, modal_step, 0)

    def local_step(block, carry):
        lanes = pl.ds(pl.multiple_of(block * LANES, LANES), LANES)
        part = block // (QUARTER // LANES)
        inner = pl.ds(pl.multiple_of(lax.rem(block, QUARTER // LANES) * LANES, LANES), LANES)
        for branch in range(3):
            filtered = (back_local if branch else conv_local)[:, lanes]
            value = filtered * partner(branch, lanes)
            for tap_at, moved in enumerate(moved_rows(branch, lanes)):
                at = branch * 3 + tap_at
                l_send[part, at : at + 1, inner] = jnp.sum(value * moved, axis=0, keepdims=True)
        l_send[part, 9:17, inner] = res_local[:, lanes]
        return carry

    lax.fori_loop(0, BLOCKS, local_step, 0)
    for step in range(1, NY):
        y_copy(l_send, l_recv, step, 9).start()
    l_recv[y] = l_send[y]

    settle(z_recv, NZ - 1, 1)

    start = jnp.zeros((MODES, QUARTER), F32)
    finish = jnp.zeros((MODES, QUARTER), F32)
    for index in range(NZ):
        start = jnp.where(
            index < z, start * group_decay + unfold(z_recv[index].astype(F32)), start
        )
        other = NZ - 1 - index
        finish = jnp.where(
            other > z, finish * group_decay + unfold(z_recv[other].astype(F32)), finish
        )
    for index in range(NY):
        b_send[index, 0:8] = start
        start = start * step_decay + y_recv[index, 0:8]
        other = NY - 1 - index
        b_send[other, 8:16] = finish
        finish = finish * step_decay + y_recv[other, 8:16]

    for step in range(1, NY):
        y_copy(b_send, b_recv, step, 2).start()
    b_recv[y] = b_send[y]

    one = jnp.exp(-speeds)
    gains = jnp.sqrt(1.0 - jnp.exp(-2.0 * speeds))
    mine = pl.ds(pl.multiple_of(y * QUARTER, QUARTER), QUARTER)
    own_columns = residue_ref[:, mine] * gains
    settle(m_recv, NY - 1, 8)
    settle(l_recv, NY - 1, 9)
    local = l_recv[0]
    for index in range(1, NY):
        local = local + l_recv[index]
    pairs = jnp.zeros((MODES, QUARTER), F32)
    for index in range(NY):
        pairs = pairs + b_send[index, 0:8] * y_recv[index, 8:16]
    res_part = gains * (local[9:17] + one * pairs)
    for branch in range(3):
        half = slice(8, 16) if branch else slice(0, 8)
        for tap_at in range(3):
            at = branch * 3 + tap_at
            pairs = jnp.zeros((MODES, QUARTER), F32)
            for index in range(NY):
                pairs = pairs + b_send[index, half] * m_recv[index, at].astype(F32)
            row = local[at : at + 1] + jnp.sum(own_columns * pairs, axis=0, keepdims=True)
            for offset in range(NDP // 2):
                r_send[2 * offset, at : at + 1] = row[:, offset * LANES : (offset + 1) * LANES]
    for offset in range(NDP // 2):
        r_send[2 * offset + 1, 0:8] = res_part[:, offset * LANES : (offset + 1) * LANES]
        r_send[2 * offset + 1, 8:9] = jnp.zeros((1, LANES), F32)

    for step in range(1, NDP):
        peer = lax.rem(dp + step, NDP)
        pltpu.make_async_remote_copy(
            src_ref=r_send.at[peer],
            dst_ref=r_recv.at[dp],
            send_sem=send_sems.at[3],
            recv_sem=recv_sems.at[3],
            device_id={"dp": peer},
            device_id_type=MESH,
        ).start()
    r_recv[dp] = r_send[dp]
    settle(r_recv, NDP - 1, 3)
    total = r_recv[0]
    for index in range(1, NDP):
        total = total + r_recv[index]
    p_send[...] = total
    p_recv[z] = total

    core = lax.rem(dp, 2)
    block_here = y * (NDP // 2) + dp // 2
    res_home = jnp.logical_and(core == 1, block_here == z)

    def line_copy(peer):
        return pltpu.make_async_remote_copy(
            src_ref=p_send,
            dst_ref=p_recv.at[z],
            send_sem=send_sems.at[4],
            recv_sem=recv_sems.at[4],
            device_id={"ctx": peer * NY + y},
            device_id_type=MESH,
        )

    @pl.when(core == 0)
    def _():
        def line_start(step, carry):
            line_copy(lax.rem(z + step, NZ)).start()
            return carry

        lax.fori_loop(1, NZ, line_start, 0)

    @pl.when(jnp.logical_and(core == 1, block_here != z))
    def _():
        line_copy(block_here).start()

    settle(b_recv, NY - 1, 2)

    for part in range(NY):
        lanes = slice(part * QUARTER, (part + 1) * QUARTER)
        columns = residue_ref[:, lanes] * gains
        state = b_recv[part, 0:8]
        costate = b_recv[part, 8:16]
        for slot, value in ((0, columns * state), (1, columns * costate)):
            high, low = split_bf16(value)
            enter[slot, :, lanes] = jnp.concatenate([high, low, high, low], axis=0).astype(BF16)
        out_state = state * step_decay + ends[0:8, lanes]
        next_first = one * out_state + tail_gd[0:1, lanes]
        next_second = one * next_first + tail_gd[1:2, lanes]
        back_second = (costate - tail_gd[8:9, lanes]) / one
        edge[0:8, lanes] = two_row_tile(
            jnp.sum(columns * next_first, axis=0, keepdims=True),
            jnp.sum(columns * next_second, axis=0, keepdims=True),
            0,
        )
        edge[8:16, lanes] = two_row_tile(
            jnp.sum(columns * costate, axis=0, keepdims=True),
            jnp.sum(columns * back_second, axis=0, keepdims=True),
            0,
        )

    lane_at = lax.broadcasted_iota(jnp.int32, (ROWS, 4 * MODES), 1)
    lane_rate = jnp.zeros((ROWS, 4 * MODES), F32)
    for mode in range(MODES):
        lane_rate = jnp.where(lax.rem(lane_at, MODES) == mode, rate_ref[mode], lane_rate)
    place = lax.broadcasted_iota(jnp.int32, (ROWS, 4 * MODES), 0).astype(F32)

    def spread(offsets):
        high, low = split_bf16(jnp.exp(-lane_rate * offsets))
        return jnp.where(lane_at < 2 * MODES, high, low).astype(BF16)

    spread_fwd = spread(place + 1.0)
    spread_back = spread(ROWS - place)
    outs = (gq_ref, gk_ref, gv_ref)

    def final_step(block, carry):
        lanes = pl.ds(pl.multiple_of(block * LANES, LANES), LANES)
        conv = conv_local[:, lanes] + jnp.dot(
            spread_fwd, enter[0, :, lanes], preferred_element_type=F32
        )
        back = back_local[:, lanes] + jnp.dot(
            spread_back, enter[1, :, lanes], preferred_element_type=F32
        )
        conv_ext = jnp.concatenate([conv, edge[0:8, lanes]], axis=0)
        back_ext = jnp.concatenate([back, edge[8:16, lanes]], axis=0)
        cot = jnp.concatenate([go_ref[:, lanes].astype(F32), after_tile(3, lanes)], axis=0)
        mixed_ref[:, lanes] = (short_q[0:ROWS, lanes] * conv).astype(BF16)
        d_shorts = (cot * conv_ext, back_ext * short_v[:, lanes], back_ext * short_k[:, lanes])
        for branch in range(3):
            value = d_shorts[branch]
            first, second, third = taps(branch, lanes)
            total = (
                first * value[:ROWS]
                + second * pltpu.roll(value, ROWS + 8 - 1, 0)[:ROWS]
                + third * pltpu.roll(value, ROWS + 8 - 2, 0)[:ROWS]
            )
            outs[branch][:, lanes] = total.astype(BF16)
        return carry

    lax.fori_loop(0, BLOCKS, final_step, 0)
    stores = [
        pltpu.make_async_copy(source, target, store_sems.at[index])
        for index, (source, target) in enumerate(
            ((mixed_ref, mixed_hbm), (gq_ref, gq_hbm), (gk_ref, gk_hbm), (gv_ref, gv_hbm))
        )
    ]
    for store in stores:
        store.start()

    def await_line():
        done = pltpu.make_async_remote_copy(
            src_ref=p_recv.at[pl.ds(0, NZ - 1)],
            dst_ref=p_recv.at[pl.ds(0, NZ - 1)],
            send_sem=send_sems.at[4],
            recv_sem=recv_sems.at[4],
            device_id={"ctx": lax.rem(z + 1, NZ) * NY + y},
            device_id_type=MESH,
        )
        done.wait_recv()
        total = p_recv[0]
        for index in range(1, NZ):
            total = total + p_recv[index]
        return total

    def share_copy(source, target, slot, peer):
        peer_y, peer_dp = plane_peer(peer)
        return pltpu.make_async_remote_copy(
            src_ref=source,
            dst_ref=target,
            send_sem=send_sems.at[slot],
            recv_sem=recv_sems.at[slot],
            device_id={"ctx": z * NY + peer_y, "dp": peer_dp},
            device_id_type=MESH,
        )

    def share(source, target, slot):
        def start_one(step, carry):
            share_copy(source, target, slot, lax.rem(plane + step, PLANE)).start()
            return carry

        lax.fori_loop(1, PLANE, start_one, 0)

    @pl.when(core == 0)
    def _():
        short_sum[block_here] = await_line()
        share(short_sum.at[block_here], short_sum.at[block_here], 5)

    @pl.when(res_home)
    def _():
        res_sum[...] = await_line()
        share(res_sum, res_sum, 10)

    def await_short(number):
        here = short_sum.at[pl.ds(0, number)]
        next_peer = lax.rem(plane + 1, PLANE)
        share_copy(here, here, 5, next_peer).wait_recv()

    @pl.when(core == 0)
    def _():
        await_short(BLOCKS - 1)

    @pl.when(core == 1)
    def _():
        await_short(BLOCKS)

    @pl.when(jnp.logical_not(res_home))
    def _():
        share_copy(res_sum, res_sum, 10, lax.rem(plane + 1, PLANE)).wait_recv()

    for block in range(BLOCKS):
        lanes = slice(block * LANES, (block + 1) * LANES)
        for branch in range(3):
            gshort_ref[branch, :, lanes] = short_sum[block, 3 * branch : 3 * branch + 3]
    gres_ref[...] = pltpu.roll(res_sum[0:8], lax.rem(LANES - 32 * y, LANES), 1)[:, :32]
    for store in stores:
        store.wait()
    for copy in halos + leaving:
        copy.wait_send()

    @pl.when(core == 0)
    def _():
        def line_end(step, carry):
            line_copy(lax.rem(z + step, NZ)).wait_send()
            return carry

        def share_end(step, carry):
            here = short_sum.at[block_here]
            share_copy(here, here, 5, lax.rem(plane + step, PLANE)).wait_send()
            return carry

        lax.fori_loop(1, NZ, line_end, 0)
        lax.fori_loop(1, PLANE, share_end, 0)

    @pl.when(jnp.logical_and(core == 1, block_here != z))
    def _():
        line_copy(block_here).wait_send()

    @pl.when(res_home)
    def _():
        def share_end(step, carry):
            share_copy(res_sum, res_sum, 10, lax.rem(plane + step, PLANE)).wait_send()
            return carry

        lax.fori_loop(1, PLANE, share_end, 0)


def store_kernel(*refs):
    sources, targets, stages = refs[:6], refs[6:12], refs[12:18]
    load_sems, store_sems = refs[18:]
    loads = [
        pltpu.make_async_copy(source, stage, load_sems.at[index])
        for index, (source, stage) in enumerate(zip(sources, stages))
    ]
    stores = [
        pltpu.make_async_copy(stage, target, store_sems.at[index])
        for index, (stage, target) in enumerate(zip(stages, targets))
    ]
    for load in loads:
        load.start()
    for load, store in zip(loads, stores):
        load.wait()
        store.start()
    for store in stores:
        store.wait()


def shards(q_in, k_in, v_in, grad_out, short_filter, residue, rate):
    inputs = (q_in[0], k_in[0], v_in[0], grad_out[0])
    vmem = pl.BlockSpec(memory_space=pltpu.VMEM)
    smem = pl.BlockSpec(memory_space=pltpu.SMEM)
    hbm = pl.BlockSpec(memory_space=pltpu.HBM)
    block = jax.ShapeDtypeStruct((ROWS, CHANNELS), BF16)
    results = pl.pallas_call(
        operator_kernel,
        out_shape=(
            block,
            block,
            block,
            block,
            jax.ShapeDtypeStruct((MODES, 32), F32),
            jax.ShapeDtypeStruct((3, 3, CHANNELS), F32),
        ),
        in_specs=[smem] + [hbm] * 4 + [vmem] * 2,
        out_specs=(hbm,) * 4 + (vmem,) * 2,
        scratch_shapes=[pltpu.VMEM((ROWS, CHANNELS), BF16)] * 8
        + [pltpu.VMEM((8, CHANNELS), BF16)] * 4
        + [
            pltpu.VMEM((ROWS + 8, CHANNELS), F32),
            pltpu.VMEM((ROWS + 8, CHANNELS), F32),
            pltpu.VMEM((ROWS + 8, CHANNELS), F32),
            pltpu.VMEM((ROWS, CHANNELS), BF16),
            pltpu.VMEM((ROWS, CHANNELS), BF16),
            pltpu.VMEM((16, CHANNELS), F32),
            pltpu.VMEM((MODES * ROWS, 2 * ROWS), BF16),
            pltpu.VMEM((MODES * ROWS, 2 * ROWS), BF16),
            pltpu.VMEM((MODES * ROWS, WIDE), F32),
            pltpu.VMEM((ROWS, CHANNELS), F32),
            pltpu.VMEM((ROWS, CHANNELS), F32),
            pltpu.VMEM((MODES, CHANNELS), F32),
            pltpu.VMEM((16, CHANNELS), F32),
            pltpu.VMEM((NY, 16, QUARTER), F32),
            pltpu.VMEM((NY, 16, QUARTER), F32),
            pltpu.VMEM((2, 16, QUARTER // 2), BF16),
            pltpu.VMEM((NZ, 16, QUARTER // 2), BF16),
            pltpu.VMEM((NY, 16, QUARTER), F32),
            pltpu.VMEM((NY, 16, QUARTER), F32),
            pltpu.VMEM((2, 4 * MODES, CHANNELS), BF16),
            pltpu.VMEM((16, CHANNELS), F32),
            pltpu.VMEM((NY, 9, MODES, QUARTER), BF16),
            pltpu.VMEM((NY, 9, MODES, QUARTER), BF16),
            pltpu.VMEM((NY, 17, QUARTER), F32),
            pltpu.VMEM((NY, 17, QUARTER), F32),
            pltpu.VMEM((NDP, 9, LANES), F32),
            pltpu.VMEM((NDP, 9, LANES), F32),
            pltpu.VMEM((9, LANES), F32),
            pltpu.VMEM((NZ, 9, LANES), F32),
            pltpu.VMEM((BLOCKS, 9, LANES), F32),
            pltpu.VMEM((9, LANES), F32),
            pltpu.SemaphoreType.DMA((4,)),
            pltpu.SemaphoreType.DMA((4,)),
            pltpu.SemaphoreType.DMA((11,)),
            pltpu.SemaphoreType.DMA((11,)),
        ],
        name="operator",
        compiler_params=pltpu.CompilerParams(
            collective_id=0, has_side_effects=True, vmem_limit_bytes=GRANT
        ),
    )(rate, *inputs, short_filter, residue.T)
    mixed, gq, gk, gv, gres, gshort = pl.pallas_call(
        store_kernel,
        out_shape=tuple(jax.ShapeDtypeStruct(item.shape, item.dtype) for item in results),
        in_specs=[hbm] * 6,
        out_specs=(hbm,) * 6,
        scratch_shapes=[pltpu.VMEM(item.shape, item.dtype) for item in results]
        + [pltpu.SemaphoreType.DMA((6,))] * 2,
        name="store",
        compiler_params=pltpu.CompilerParams(vmem_limit_bytes=GRANT),
    )(*results)
    return (
        mixed[None],
        gq[None],
        gk[None],
        gv[None],
        gres.T,
        gshort,
    )


def solution(mesh):
    placed = P("dp", "ctx", None)
    return jax.shard_map(
        shards,
        mesh=mesh,
        in_specs=(placed, placed, placed, placed, P(), P(), P()),
        out_specs=(placed, placed, placed, placed, P("ctx", None), P()),
        check_vma=False,
    )
```

time: 84.6 us -> 58.2 us (0.69)
  local copies, waits for them, and re-layouts: 11.8 us -> 0 us
  Pallas kernels: 64.6 us -> 57.3 us
  starting transfers between devices: 5.95 us -> 0 us
  waiting for transfers between devices: 0.93 us -> 0 us
    pallas_call x1, Pallas kernels: 64.6 us -> 54.8 us  [shards(): pl.pallas_call(operator_kernel, out_shape=(block, block, block, block, ja...]
    unnamed x19 -> x0, local copies, waits for them, and re-layouts: 8.66 us -> none
    ppermute x2 -> x0, starting transfers between devices: 5.95 us -> none  [the longest x1 4.66 us: shards(): before = lax.ppermute(tails, 'ctx', [(i, i + 1) for i in range(count - 1)])]
    pallas_call x0 -> x1, Pallas kernels: none -> 2.48 us  [shards(): pl.pallas_call(store_kernel, out_shape=tuple((jax.ShapeDtypeStruct(item.s...]
    slice x3 -> x0, local copies, waits for them, and re-layouts: 2.43 us -> none  [shards(): heads = jnp.stack([item[:2] for item in inputs])]
    ppermute x2 -> x0, waiting for transfers between devices: 0.93 us -> none  [the longest x1 0.93 us: shards(): before = lax.ppermute(tails, 'ctx', [(i, i + 1) for i in range(count - 1)])]
  transfers between devices with their start and end apart: 2 -> 0, of which waited for: 1 -> 0; matrix products, arithmetic and copies ran while one was open for 0% -> 0% of each run, Pallas kernels for 0% -> 0%
where the time goes in v2:
time: 58.2 us; the launch traced here: 58 us
  Pallas kernels  57.3 us (98%)
  between operations  0.64 us (1%)
    pallas_call x1, Pallas kernels, shards(): pl.pallas_call(operator_kernel, out_shape=(block, block, block, block, ja...  54.8 us
    pallas_call x1, Pallas kernels, shards(): pl.pallas_call(store_kernel, out_shape=tuple((jax.ShapeDtypeStruct(item.s...  2.48 us

profile of v2, /device:TPU:1, one launch (start us, length us, event | category | flops | bytes accessed | tf_op | source)
XLA Modules:
  0.0 58.0 jit_solution(10834910276850032903)
XLA Ops:
  0.6 54.8 %operator.1 = (bf16[128,2048]{1,0:T(8,128)(2,1)}, bf16[128,2048]{1,0:T(8,128)(2,1)}, bf16[128,2048]{1,0:T(8,128)(2,1)}, bf16[128,2048]{1,0:T(8,128)(2,1)}, f32[8,32]{1,0:T(8,128)}, /*index=5*/f32[3,3,2048]{2,1,0:T(4,128)}) custom-call(f32[8]{0:T(128)} %rate_ref.1, bf16[128,2048]{1,0:T(8,128)(2,1)} %bitcast.10, bf16[128,2048]{1,0:T(8,128)(2,1)} %bitcast.11, ...), custom_call_target="tpu_custom_call" | custom-call | tf_op jit(solution)/shard_map/operator/pallas_call | solution.py:713
  55.5 2.5 %store.1 = (bf16[128,2048]{1,0:T(8,128)(2,1)}, bf16[128,2048]{1,0:T(8,128)(2,1)}, bf16[128,2048]{1,0:T(8,128)(2,1)}, bf16[128,2048]{1,0:T(8,128)(2,1)}, f32[8,32]{1,0:T(8,128)}, /*index=5*/f32[3,3,2048]{2,1,0:T(4,128)}) custom-call(bf16[128,2048]{1,0:T(8,128)(2,1)} %get-tuple-element.18.refs_0_, bf16[128,2048]{1,0:T(8,128)(2,1)} %get-tuple-element.19.refs_1_, ...), custom_call_target="tpu_custom_call" | custom-call | tf_op jit(solution)/shard_map/store/pallas_call | solution.py:769

commit v3 on v2

--- a/solution.py
+++ b/solution.py
@@ -43,8 +43,19 @@
     return total
 
 
-def plane_peer(index):
-    return index // NDP, lax.rem(index, NDP)
+def farthest_first(index):
+    half = (index + 1) // 2
+    return NZ // 2 + half * (1 - 2 * lax.rem(index, 2))
+
+
+PLANE_STEPS = [
+    (dy, dx, core)
+    for dy, dx, core in sorted(
+        ((dy, dx, core) for dy in range(NY) for dx in range(NDP // 2) for core in range(2)),
+        key=lambda at: (-min(at[0], NY - at[0]) - min(at[1], NDP // 2 - at[1]), at),
+    )
+    if (dy, dx, core) != (0, 0, 0)
+]
 
 
 def operator_kernel(
@@ -113,7 +124,6 @@
     dp = lax.axis_index("dp")
     z = ctx // NY
     y = lax.rem(ctx, NY)
-    plane = y * NDP + dp
 
     inputs = (q_ref, k_ref, v_ref, go_ref)
     loads = [
@@ -127,33 +137,47 @@
     count = NZ * NY
     following = lax.rem(ctx + 1, count)
     preceding = lax.rem(ctx + count - 1, count)
+    column = dp // 2
+    core = lax.rem(dp, 2)
+
+    def line_peer(index):
+        return lax.rem(z + farthest_first(index), NZ)
+
+    def plane_device(step):
+        dy, dx, dcore = step
+        peer_x = lax.rem(column + dx, NDP // 2)
+        peer_core = (1 - core) if dcore else core
+        return {"ctx": z * NY + lax.rem(y + dy, NY), "dp": peer_x * 2 + peer_core}
+
+    def greet_line(index, carry):
+        pl.semaphore_signal(
+            barrier, inc=1, device_id={"ctx": line_peer(index) * NY + y}, device_id_type=MESH
+        )
+        return carry
+
+    lax.fori_loop(0, NZ - 1, greet_line, 0)
+    for step in PLANE_STEPS:
+        pl.semaphore_signal(
+            barrier, inc=1, device_id=plane_device(step), device_id_type=MESH
+        )
     for neighbour in (following, preceding):
         pl.semaphore_signal(
             barrier, inc=1, device_id={"ctx": neighbour}, device_id_type=MESH
         )
 
-    def greet_line(step, carry):
-        peer = lax.rem(z + step, NZ)
-        pl.semaphore_signal(
-            barrier, inc=1, device_id={"ctx": peer * NY + y}, device_id_type=MESH
-        )
-        return carry
-
-    def greet_plane(step, carry):
-        peer_y, peer_dp = plane_peer(lax.rem(plane + step, PLANE))
-        pl.semaphore_signal(
-            barrier,
-            inc=1,
-            device_id={"ctx": z * NY + peer_y, "dp": peer_dp},
-            device_id_type=MESH,
-        )
-        return carry
-
-    lax.fori_loop(1, NZ, greet_line, 0)
-    lax.fori_loop(1, PLANE, greet_plane, 0)
-
     def taps(branch, lanes):
         return [filter_ref[branch, j : j + 1, lanes] for j in range(3)]
+
+    row_at = lax.broadcasted_iota(jnp.int32, (ROWS, ROWS), 0)
+    col_at = lax.broadcasted_iota(jnp.int32, (ROWS, ROWS), 1)
+    for mode in range(MODES):
+        speed = rate_ref[mode]
+        here = slice(mode * ROWS, (mode + 1) * ROWS)
+        for table, lag in ((fwd_table, row_at - col_at), (bwd_table, col_at - row_at)):
+            power = jnp.exp(-speed * jnp.maximum(lag, 0).astype(F32))
+            high, low = split_bf16(jnp.where(lag >= 0, power, 0.0))
+            table[here, 0:ROWS] = high.astype(BF16)
+            table[here, ROWS : 2 * ROWS] = low.astype(BF16)
 
     for load in loads:
         load.wait()
@@ -341,8 +365,8 @@
     z_send[0] = fold(ahead_total).astype(BF16)
     z_send[1] = fold(back_total).astype(BF16)
 
-    def z_start(step, carry):
-        peer = lax.rem(z + step, NZ)
+    def z_start(index, carry):
+        peer = line_peer(index)
         pltpu.make_async_remote_copy(
             src_ref=z_send.at[jnp.where(peer < z, 1, 0)],
             dst_ref=z_recv.at[z],
@@ -353,22 +377,11 @@
         ).start()
         return carry
 
-    lax.fori_loop(1, NZ, z_start, 0)
+    lax.fori_loop(0, NZ - 1, z_start, 0)
     z_recv[z] = jnp.zeros((16, QUARTER // 2), BF16)
     for step in range(1, NY):
         y_copy(m_send, m_recv, step, 8).start()
     m_recv[y] = m_send[y]
-
-    row_at = lax.broadcasted_iota(jnp.int32, (ROWS, ROWS), 0)
-    col_at = lax.broadcasted_iota(jnp.int32, (ROWS, ROWS), 1)
-    for mode in range(MODES):
-        speed = rate_ref[mode]
-        here = slice(mode * ROWS, (mode + 1) * ROWS)
-        for table, lag in ((fwd_table, row_at - col_at), (bwd_table, col_at - row_at)):
-            power = jnp.exp(-speed * jnp.maximum(lag, 0).astype(F32))
-            high, low = split_bf16(jnp.where(lag >= 0, power, 0.0))
-            table[here, 0:ROWS] = high.astype(BF16)
-            table[here, ROWS : 2 * ROWS] = low.astype(BF16)
 
     gain_rows = jnp.sqrt(1.0 - jnp.exp(-2.0 * rate_rows(rate_ref, WIDE)))
 
@@ -404,21 +417,31 @@
 
     def local_step(block, carry):
         lanes = pl.ds(pl.multiple_of(block * LANES, LANES), LANES)
-        part = block // (QUARTER // LANES)
-        inner = pl.ds(pl.multiple_of(lax.rem(block, QUARTER // LANES) * LANES, LANES), LANES)
         for branch in range(3):
             filtered = (back_local if branch else conv_local)[:, lanes]
             value = filtered * partner(branch, lanes)
             for tap_at, moved in enumerate(moved_rows(branch, lanes)):
                 at = branch * 3 + tap_at
-                l_send[part, at : at + 1, inner] = jnp.sum(value * moved, axis=0, keepdims=True)
-        l_send[part, 9:17, inner] = res_local[:, lanes]
+                l_send[2 * block, at : at + 1] = jnp.sum(value * moved, axis=0, keepdims=True)
+        l_send[2 * block + 1, 0:8] = res_local[:, lanes] * gain_rows[:, :LANES]
+        l_send[2 * block + 1, 8:9] = jnp.zeros((1, LANES), F32)
         return carry
 
     lax.fori_loop(0, BLOCKS, local_step, 0)
-    for step in range(1, NY):
-        y_copy(l_send, l_recv, step, 9).start()
-    l_recv[y] = l_send[y]
+
+    plane = y * NDP + dp
+    for step in PLANE_STEPS:
+        where = plane_device(step)
+        piece = lax.rem(y + step[0], NY) * NDP + where["dp"]
+        pltpu.make_async_remote_copy(
+            src_ref=l_send.at[piece],
+            dst_ref=l_recv.at[plane],
+            send_sem=send_sems.at[9],
+            recv_sem=recv_sems.at[9],
+            device_id=where,
+            device_id_type=MESH,
+        ).start()
+    l_recv[plane] = l_send[plane]
 
     settle(z_recv, NZ - 1, 1)
 
@@ -448,14 +471,10 @@
     mine = pl.ds(pl.multiple_of(y * QUARTER, QUARTER), QUARTER)
     own_columns = residue_ref[:, mine] * gains
     settle(m_recv, NY - 1, 8)
-    settle(l_recv, NY - 1, 9)
-    local = l_recv[0]
-    for index in range(1, NY):
-        local = local + l_recv[index]
     pairs = jnp.zeros((MODES, QUARTER), F32)
     for index in range(NY):
         pairs = pairs + b_send[index, 0:8] * y_recv[index, 8:16]
-    res_part = gains * (local[9:17] + one * pairs)
+    res_part = gains * one * pairs
     for branch in range(3):
         half = slice(8, 16) if branch else slice(0, 8)
         for tap_at in range(3):
@@ -463,7 +482,7 @@
             pairs = jnp.zeros((MODES, QUARTER), F32)
             for index in range(NY):
                 pairs = pairs + b_send[index, half] * m_recv[index, at].astype(F32)
-            row = local[at : at + 1] + jnp.sum(own_columns * pairs, axis=0, keepdims=True)
+            row = jnp.sum(own_columns * pairs, axis=0, keepdims=True)
             for offset in range(NDP // 2):
                 r_send[2 * offset, at : at + 1] = row[:, offset * LANES : (offset + 1) * LANES]
     for offset in range(NDP // 2):
@@ -482,14 +501,16 @@
         ).start()
     r_recv[dp] = r_send[dp]
     settle(r_recv, NDP - 1, 3)
+    settle(l_recv, PLANE - 1, 9)
     total = r_recv[0]
     for index in range(1, NDP):
         total = total + r_recv[index]
+    for index in range(PLANE):
+        total = total + l_recv[index]
     p_send[...] = total
     p_recv[z] = total
 
-    core = lax.rem(dp, 2)
-    block_here = y * (NDP // 2) + dp // 2
+    block_here = y * (NDP // 2) + column
     res_home = jnp.logical_and(core == 1, block_here == z)
 
     def line_copy(peer):
@@ -504,11 +525,11 @@
 
     @pl.when(core == 0)
     def _():
-        def line_start(step, carry):
-            line_copy(lax.rem(z + step, NZ)).start()
+        def line_start(index, carry):
+            line_copy(line_peer(index)).start()
             return carry
 
-        lax.fori_loop(1, NZ, line_start, 0)
+        lax.fori_loop(0, NZ - 1, line_start, 0)
 
     @pl.when(jnp.logical_and(core == 1, block_here != z))
     def _():
@@ -602,23 +623,19 @@
             total = total + p_recv[index]
         return total
 
-    def share_copy(source, target, slot, peer):
-        peer_y, peer_dp = plane_peer(peer)
+    def share_copy(source, target, slot, step):
         return pltpu.make_async_remote_copy(
             src_ref=source,
             dst_ref=target,
             send_sem=send_sems.at[slot],
             recv_sem=recv_sems.at[slot],
-            device_id={"ctx": z * NY + peer_y, "dp": peer_dp},
+            device_id=plane_device(step),
             device_id_type=MESH,
         )
 
     def share(source, target, slot):
-        def start_one(step, carry):
-            share_copy(source, target, slot, lax.rem(plane + step, PLANE)).start()
-            return carry
-
-        lax.fori_loop(1, PLANE, start_one, 0)
+        for step in PLANE_STEPS:
+            share_copy(source, target, slot, step).start()
 
     @pl.when(core == 0)
     def _():
@@ -632,8 +649,7 @@
 
     def await_short(number):
         here = short_sum.at[pl.ds(0, number)]
-        next_peer = lax.rem(plane + 1, PLANE)
-        share_copy(here, here, 5, next_peer).wait_recv()
+        share_copy(here, here, 5, PLANE_STEPS[0]).wait_recv()
 
     @pl.when(core == 0)
     def _():
@@ -645,7 +661,7 @@
 
     @pl.when(jnp.logical_not(res_home))
     def _():
-        share_copy(res_sum, res_sum, 10, lax.rem(plane + 1, PLANE)).wait_recv()
+        share_copy(res_sum, res_sum, 10, PLANE_STEPS[0]).wait_recv()
 
     for block in range(BLOCKS):
         lanes = slice(block * LANES, (block + 1) * LANES)
@@ -659,17 +675,17 @@
 
     @pl.when(core == 0)
     def _():
-        def line_end(step, carry):
-            line_copy(lax.rem(z + step, NZ)).wait_send()
-            return carry
-
-        def share_end(step, carry):
-            here = short_sum.at[block_here]
-            share_copy(here, here, 5, lax.rem(plane + step, PLANE)).wait_send()
-            return carry
-
-        lax.fori_loop(1, NZ, line_end, 0)
-        lax.fori_loop(1, PLANE, share_end, 0)
+        here = p_recv.at[pl.ds(0, NZ - 1)]
+        pltpu.make_async_remote_copy(
+            src_ref=here,
+            dst_ref=here,
+            send_sem=send_sems.at[4],
+            recv_sem=recv_sems.at[4],
+            device_id={"ctx": line_peer(0) * NY + y},
+            device_id_type=MESH,
+        ).wait_send()
+        for step in PLANE_STEPS:
+            share_copy(short_sum.at[block_here], short_sum.at[block_here], 5, step).wait_send()
 
     @pl.when(jnp.logical_and(core == 1, block_here != z))
     def _():
@@ -677,23 +693,24 @@
 
     @pl.when(res_home)
     def _():
-        def share_end(step, carry):
-            share_copy(res_sum, res_sum, 10, lax.rem(plane + step, PLANE)).wait_send()
-            return carry
-
-        lax.fori_loop(1, PLANE, share_end, 0)
+        for step in PLANE_STEPS:
+            share_copy(res_sum, res_sum, 10, step).wait_send()
 
 
 def store_kernel(*refs):
     sources, targets, stages = refs[:6], refs[6:12], refs[12:18]
     load_sems, store_sems = refs[18:]
+    pieces = []
+    for source, target, stage in zip(sources, targets, stages):
+        rows = source.shape[0]
+        for first in range(0, source.shape[0], rows):
+            here = pl.ds(first, rows)
+            pieces.append((source.at[here], stage.at[here], target.at[here], len(pieces)))
     loads = [
-        pltpu.make_async_copy(source, stage, load_sems.at[index])
-        for index, (source, stage) in enumerate(zip(sources, stages))
+        pltpu.make_async_copy(source, stage, load_sems.at[at]) for source, stage, _, at in pieces
     ]
     stores = [
-        pltpu.make_async_copy(stage, target, store_sems.at[index])
-        for index, (stage, target) in enumerate(zip(stages, targets))
+        pltpu.make_async_copy(stage, target, store_sems.at[at]) for _, stage, target, at in pieces
     ]
     for load in loads:
         load.start()
@@ -748,8 +765,8 @@
             pltpu.VMEM((16, CHANNELS), F32),
             pltpu.VMEM((NY, 9, MODES, QUARTER), BF16),
             pltpu.VMEM((NY, 9, MODES, QUARTER), BF16),
-            pltpu.VMEM((NY, 17, QUARTER), F32),
-            pltpu.VMEM((NY, 17, QUARTER), F32),
+            pltpu.VMEM((PLANE, 9, LANES), F32),
+            pltpu.VMEM((PLANE, 9, LANES), F32),
             pltpu.VMEM((NDP, 9, LANES), F32),
             pltpu.VMEM((NDP, 9, LANES), F32),
             pltpu.VMEM((9, LANES), F32),

time: 58.2 us -> 54.9 us (0.943)
  Pallas kernels: 57.3 us -> 54 us
    pallas_call x1, Pallas kernels: 54.8 us -> 51.5 us  [shards(): pl.pallas_call(operator_kernel, out_shape=(block, block, block, block, ja...]
where the time goes in v3:
time: 54.9 us; the launch traced here: 54.6 us
  Pallas kernels  54 us (98%)
  between operations  0.64 us (1%)
    pallas_call x1, Pallas kernels, shards(): pl.pallas_call(operator_kernel, out_shape=(block, block, block, block, ja...  51.5 us
    pallas_call x1, Pallas kernels, shards(): pl.pallas_call(store_kernel, out_shape=tuple((jax.ShapeDtypeStruct(item.s...  2.48 us

profile of v3, /device:TPU:1, one launch (start us, length us, event | category | flops | bytes accessed | tf_op | source)
XLA Modules:
  0.0 54.6 jit_solution(5537723279053341662)
XLA Ops:
  0.6 51.5 %operator.1 = (bf16[128,2048]{1,0:T(8,128)(2,1)}, bf16[128,2048]{1,0:T(8,128)(2,1)}, bf16[128,2048]{1,0:T(8,128)(2,1)}, bf16[128,2048]{1,0:T(8,128)(2,1)}, f32[8,32]{1,0:T(8,128)}, /*index=5*/f32[3,3,2048]{2,1,0:T(4,128)}) custom-call(f32[8]{0:T(128)} %rate_ref.1, bf16[128,2048]{1,0:T(8,128)(2,1)} %bitcast.10, bf16[128,2048]{1,0:T(8,128)(2,1)} %bitcast.11, ...), custom_call_target="tpu_custom_call" | custom-call | tf_op jit(solution)/shard_map/operator/pallas_call | solution.py:730
  52.2 2.5 %store.1 = (bf16[128,2048]{1,0:T(8,128)(2,1)}, bf16[128,2048]{1,0:T(8,128)(2,1)}, bf16[128,2048]{1,0:T(8,128)(2,1)}, bf16[128,2048]{1,0:T(8,128)(2,1)}, f32[8,32]{1,0:T(8,128)}, /*index=5*/f32[3,3,2048]{2,1,0:T(4,128)}) custom-call(bf16[128,2048]{1,0:T(8,128)(2,1)} %get-tuple-element.18.refs_0_, bf16[128,2048]{1,0:T(8,128)(2,1)} %get-tuple-element.19.refs_1_, ...), custom_call_target="tpu_custom_call" | custom-call | tf_op jit(solution)/shard_map/store/pallas_call | solution.py:786

commit v4 on v3

--- a/solution.py
+++ b/solution.py
@@ -105,6 +105,9 @@
     b_recv,
     enter,
     edge,
+    e_send,
+    e_recv,
+    e_prev,
     m_send,
     m_recv,
     l_send,
@@ -165,6 +168,11 @@
             barrier, inc=1, device_id={"ctx": neighbour}, device_id_type=MESH
         )
 
+    @pl.when(jnp.logical_or(y == 1, y == 2))
+    def _():
+        sender = lax.rem(z + NZ - 1, NZ) * NY + NY - 1
+        pl.semaphore_signal(barrier, inc=1, device_id={"ctx": sender}, device_id_type=MESH)
+
     def taps(branch, lanes):
         return [filter_ref[branch, j : j + 1, lanes] for j in range(3)]
 
@@ -195,24 +203,9 @@
                 tails = jnp.where(here, last[14 + index : 15 + index], tails)
     tail_send[...] = tails.astype(BF16)
     head_send[...] = heads.astype(BF16)
-
-    pl.semaphore_wait(barrier, NZ - 1 + PLANE - 1 + 2)
-    halos = [
-        pltpu.make_async_remote_copy(
-            src_ref=source,
-            dst_ref=target,
-            send_sem=send_sems.at[slot],
-            recv_sem=recv_sems.at[slot],
-            device_id={"ctx": neighbour},
-            device_id_type=MESH,
-        )
-        for slot, source, target, neighbour in (
-            (6, tail_send, tail_recv, following),
-            (7, head_send, head_recv, preceding),
-        )
-    ]
-    for halo in halos:
-        halo.start()
+    edges = jnp.concatenate([tails, heads], axis=0).astype(BF16)
+    for part in range(NY):
+        e_send[part] = edges[:, part * QUARTER : (part + 1) * QUARTER]
 
     def before_tile(branch, lanes):
         rows = tail_recv[:, lanes].astype(F32)[2 * branch : 2 * branch + 2]
@@ -250,6 +243,181 @@
 
     lax.fori_loop(0, BLOCKS, short_step, 0)
 
+    rates = rate_rows(rate_ref, ROWS)
+    place = lax.broadcasted_iota(jnp.int32, (MODES, ROWS), 1).astype(F32)
+    def compute_ends():
+        for slot, offsets, operand in ((0, ROWS - 1.0 - place, gated), (1, place, d_conv)):
+            high, low = split_bf16(jnp.exp(-rates * offsets))
+            table = jnp.concatenate([high, low], axis=0).astype(BF16)
+            product = jnp.dot(table, operand[...], preferred_element_type=F32)
+            ends[slot * 8 : slot * 8 + 8, :] = product[:8] + product[8:]
+
+    compute_ends()
+
+    for part in range(NY):
+        y_send[part] = ends[:, part * QUARTER : (part + 1) * QUARTER]
+
+    pl.semaphore_wait(barrier, NZ - 1 + PLANE - 1 + 2 + 2 * (y // (NY - 1)))
+
+    def y_copy(source, target, step, slot):
+        peer = lax.rem(y + step, NY)
+        return pltpu.make_async_remote_copy(
+            src_ref=source.at[peer],
+            dst_ref=target.at[y],
+            send_sem=send_sems.at[slot],
+            recv_sem=recv_sems.at[slot],
+            device_id={"ctx": z * NY + peer},
+            device_id_type=MESH,
+        )
+
+    leaving = []
+
+    def settle(target, number, slot):
+        done = pltpu.make_async_remote_copy(
+            src_ref=target.at[pl.ds(0, number)],
+            dst_ref=target.at[pl.ds(0, number)],
+            send_sem=send_sems.at[slot],
+            recv_sem=recv_sems.at[slot],
+            device_id={"ctx": z * NY + lax.rem(y + 1, NY)},
+            device_id_type=MESH,
+        )
+        done.wait_recv()
+        leaving.append(done)
+
+    for step in range(1, NY):
+        y_copy(y_send, y_recv, step, 0).start()
+    y_recv[y] = y_send[y]
+    for step in range(1, NY):
+        y_copy(e_send, e_recv, step, 11).start()
+    e_recv[y] = e_send[y]
+
+    def onward_copy(part):
+        return pltpu.make_async_remote_copy(
+            src_ref=e_send.at[part],
+            dst_ref=e_prev,
+            send_sem=send_sems.at[12],
+            recv_sem=recv_sems.at[12],
+            device_id={"ctx": lax.rem(z + 1, NZ) * NY + part},
+            device_id_type=MESH,
+        )
+
+    @pl.when(y == NY - 1)
+    def _():
+        for part in range(NY):
+            onward_copy(part).start()
+
+    halos = [
+        pltpu.make_async_remote_copy(
+            src_ref=source,
+            dst_ref=target,
+            send_sem=send_sems.at[slot],
+            recv_sem=recv_sems.at[slot],
+            device_id={"ctx": neighbour},
+            device_id_type=MESH,
+        )
+        for slot, source, target, neighbour in (
+            (6, tail_send, tail_recv, following),
+            (7, head_send, head_recv, preceding),
+        )
+    ]
+    for halo in halos:
+        halo.start()
+
+    gain_rows = jnp.sqrt(1.0 - jnp.exp(-2.0 * rate_rows(rate_ref, WIDE)))
+
+    def back_step(block, carry):
+        lanes = pl.ds(pl.multiple_of(block * WIDE, WIDE), WIDE)
+        columns = residue_ref[:, lanes] * gain_rows
+        source = d_conv[:, lanes]
+        modal[...] = jnp.dot(
+            bwd_table[...],
+            jnp.concatenate([source, source], axis=0),
+            preferred_element_type=F32,
+        )
+        total = jnp.zeros((ROWS, WIDE), F32)
+        for mode in range(MODES):
+            total = total + columns[mode : mode + 1] * modal[mode * ROWS : (mode + 1) * ROWS, :]
+        back_local[:, lanes] = total
+        return carry
+
+    lax.fori_loop(0, CHANNELS // WIDE, back_step, 0)
+
+    settle(y_recv, NY - 1, 0)
+
+    speeds = rate_rows(rate_ref, QUARTER)
+    settle(e_recv, NY - 1, 11)
+    onward_copy(0).wait_recv()
+
+    mine = pl.ds(pl.multiple_of(y * QUARTER, QUARTER), QUARTER)
+    own_taps = [taps(branch, mine) for branch in range(3)]
+
+    def rounded(value):
+        return value.astype(BF16).astype(F32)
+
+    for index in range(NY):
+        here = e_recv[index].astype(F32)[8:16]
+        prior = (e_recv[index - 1] if index else e_prev[...]).astype(F32)[0:8]
+        if index == 0:
+            prior = jnp.where(z == 0, 0.0, prior)
+        plain = []
+        full = []
+        for branch in range(3):
+            first, second, third = own_taps[branch]
+            row0, row1 = (here[2 * branch + at : 2 * branch + at + 1] for at in range(2))
+            old0, old1 = (prior[2 * branch + at : 2 * branch + at + 1] for at in range(2))
+            plain.append((first * row0, first * row1 + second * row0))
+            full.append(
+                (
+                    first * row0 + second * old1 + third * old0,
+                    first * row1 + second * row0 + third * old1,
+                )
+            )
+        d_gate = []
+        d_out = []
+        for at in range(2):
+            cot = here[6 + at : 7 + at]
+            d_gate.append(
+                rounded(full[1][at] * full[2][at]) - rounded(plain[1][at] * plain[2][at])
+            )
+            d_out.append(rounded(cot * full[0][at]) - rounded(cot * plain[0][at]))
+        y_recv[index, 0:8] = (
+            y_recv[index, 0:8]
+            + jnp.exp(-speeds * (ROWS - 1.0)) * d_gate[0]
+            + jnp.exp(-speeds * (ROWS - 2.0)) * d_gate[1]
+        )
+        y_recv[index, 8:16] = y_recv[index, 8:16] + d_out[0] + jnp.exp(-speeds) * d_out[1]
+
+    step_decay = jnp.exp(-speeds * float(ROWS))
+    group_decay = jnp.exp(-speeds * float(ROWS * NY))
+
+    def fold(value):
+        return jnp.concatenate([value[:, : QUARTER // 2], value[:, QUARTER // 2 :]], axis=0)
+
+    def unfold(value):
+        return jnp.concatenate([value[:8], value[8:]], axis=1)
+
+    ahead_total = y_recv[0, 0:8]
+    back_total = y_recv[NY - 1, 8:16]
+    for index in range(1, NY):
+        ahead_total = ahead_total * step_decay + y_recv[index, 0:8]
+        back_total = back_total * step_decay + y_recv[NY - 1 - index, 8:16]
+    z_send[0] = fold(ahead_total).astype(BF16)
+    z_send[1] = fold(back_total).astype(BF16)
+
+    def z_start(index, carry):
+        peer = line_peer(index)
+        pltpu.make_async_remote_copy(
+            src_ref=z_send.at[jnp.where(peer < z, 1, 0)],
+            dst_ref=z_recv.at[z],
+            send_sem=send_sems.at[1],
+            recv_sem=recv_sems.at[1],
+            device_id={"ctx": peer * NY + y},
+            device_id_type=MESH,
+        ).start()
+        return carry
+
+    lax.fori_loop(0, NZ - 1, z_start, 0)
+    z_recv[z] = jnp.zeros((16, QUARTER // 2), BF16)
     for halo in halos:
         halo.wait_recv()
 
@@ -267,52 +435,22 @@
             nexts.append(convolve(branch, lanes, extended))
             shorts[branch][ROWS : ROWS + 8, lanes] = nexts[branch]
         gated[0:16, lanes] = (firsts[1] * firsts[2]).astype(BF16)
-        d_conv[0:16, lanes] = (go_ref[0:16, lanes].astype(F32) * firsts[0]).astype(BF16)
+        fresh = (go_ref[0:16, lanes].astype(F32) * firsts[0]).astype(BF16)
+        change = fresh.astype(F32) - d_conv[0:16, lanes].astype(F32)
+        d_conv[0:16, lanes] = fresh
+        columns = residue_ref[:, lanes] * gain_rows[:, :LANES]
+        whole = jnp.sum(columns, axis=0, keepdims=True)
+        decayed = jnp.sum(columns * jnp.exp(-rates), axis=0, keepdims=True)
+        back_local[0:8, lanes] = back_local[0:8, lanes] + two_row_tile(
+            whole * change[0:1] + decayed * change[1:2], whole * change[1:2], 0
+        )
         tail_gd[0:8, lanes] = (nexts[1] * nexts[2]).astype(BF16).astype(F32)
         tail_gd[8:16, lanes] = (after_tile(3, lanes) * nexts[0]).astype(BF16).astype(F32)
         return carry
 
     lax.fori_loop(0, BLOCKS, patch_step, 0)
 
-    rates = rate_rows(rate_ref, ROWS)
-    place = lax.broadcasted_iota(jnp.int32, (MODES, ROWS), 1).astype(F32)
-    for slot, offsets, operand in ((0, ROWS - 1.0 - place, gated), (1, place, d_conv)):
-        high, low = split_bf16(jnp.exp(-rates * offsets))
-        table = jnp.concatenate([high, low], axis=0).astype(BF16)
-        product = jnp.dot(table, operand[...], preferred_element_type=F32)
-        ends[slot * 8 : slot * 8 + 8, :] = product[:8] + product[8:]
-
-    for part in range(NY):
-        y_send[part] = ends[:, part * QUARTER : (part + 1) * QUARTER]
-
-    def y_copy(source, target, step, slot):
-        peer = lax.rem(y + step, NY)
-        return pltpu.make_async_remote_copy(
-            src_ref=source.at[peer],
-            dst_ref=target.at[y],
-            send_sem=send_sems.at[slot],
-            recv_sem=recv_sems.at[slot],
-            device_id={"ctx": z * NY + peer},
-            device_id_type=MESH,
-        )
-
-    leaving = []
-
-    def settle(target, number, slot):
-        done = pltpu.make_async_remote_copy(
-            src_ref=target.at[pl.ds(0, number)],
-            dst_ref=target.at[pl.ds(0, number)],
-            send_sem=send_sems.at[slot],
-            recv_sem=recv_sems.at[slot],
-            device_id={"ctx": z * NY + lax.rem(y + 1, NY)},
-            device_id_type=MESH,
-        )
-        done.wait_recv()
-        leaving.append(done)
-
-    for step in range(1, NY):
-        y_copy(y_send, y_recv, step, 0).start()
-    y_recv[y] = y_send[y]
+    compute_ends()
 
     place = lax.broadcasted_iota(jnp.int32, (MODES, ROWS), 1).astype(F32)
     weigh_fwd = jnp.exp(-rates * (place + 1.0)).astype(BF16)
@@ -345,45 +483,9 @@
 
     lax.fori_loop(0, CHANNELS // WIDE, moment_step, 0)
 
-    settle(y_recv, NY - 1, 0)
-
-    speeds = rate_rows(rate_ref, QUARTER)
-    step_decay = jnp.exp(-speeds * float(ROWS))
-    group_decay = jnp.exp(-speeds * float(ROWS * NY))
-
-    def fold(value):
-        return jnp.concatenate([value[:, : QUARTER // 2], value[:, QUARTER // 2 :]], axis=0)
-
-    def unfold(value):
-        return jnp.concatenate([value[:8], value[8:]], axis=1)
-
-    ahead_total = y_recv[0, 0:8]
-    back_total = y_recv[NY - 1, 8:16]
-    for index in range(1, NY):
-        ahead_total = ahead_total * step_decay + y_recv[index, 0:8]
-        back_total = back_total * step_decay + y_recv[NY - 1 - index, 8:16]
-    z_send[0] = fold(ahead_total).astype(BF16)
-    z_send[1] = fold(back_total).astype(BF16)
-
-    def z_start(index, carry):
-        peer = line_peer(index)
-        pltpu.make_async_remote_copy(
-            src_ref=z_send.at[jnp.where(peer < z, 1, 0)],
-            dst_ref=z_recv.at[z],
-            send_sem=send_sems.at[1],
-            recv_sem=recv_sems.at[1],
-            device_id={"ctx": peer * NY + y},
-            device_id_type=MESH,
-        ).start()
-        return carry
-
-    lax.fori_loop(0, NZ - 1, z_start, 0)
-    z_recv[z] = jnp.zeros((16, QUARTER // 2), BF16)
     for step in range(1, NY):
         y_copy(m_send, m_recv, step, 8).start()
     m_recv[y] = m_send[y]
-
-    gain_rows = jnp.sqrt(1.0 - jnp.exp(-2.0 * rate_rows(rate_ref, WIDE)))
 
     def modal_step(block, carry):
         lanes = pl.ds(pl.multiple_of(block * WIDE, WIDE), WIDE)
@@ -401,16 +503,6 @@
             total = total + columns[mode : mode + 1] * state
             res_local[mode : mode + 1, lanes] = jnp.sum(cot * state, axis=0, keepdims=True)
         conv_local[:, lanes] = total
-        source = d_conv[:, lanes]
-        modal[...] = jnp.dot(
-            bwd_table[...],
-            jnp.concatenate([source, source], axis=0),
-            preferred_element_type=F32,
-        )
-        total = jnp.zeros((ROWS, WIDE), F32)
-        for mode in range(MODES):
-            total = total + columns[mode : mode + 1] * modal[mode * ROWS : (mode + 1) * ROWS, :]
-        back_local[:, lanes] = total
         return carry
 
     lax.fori_loop(0, CHANNELS // WIDE, modal_step, 0)
@@ -468,7 +560,6 @@
 
     one = jnp.exp(-speeds)
     gains = jnp.sqrt(1.0 - jnp.exp(-2.0 * speeds))
-    mine = pl.ds(pl.multiple_of(y * QUARTER, QUARTER), QUARTER)
     own_columns = residue_ref[:, mine] * gains
     settle(m_recv, NY - 1, 8)
     pairs = jnp.zeros((MODES, QUARTER), F32)
@@ -672,6 +763,11 @@
         store.wait()
     for copy in halos + leaving:
         copy.wait_send()
+
+    @pl.when(y == NY - 1)
+    def _():
+        for part in range(NY):
+            onward_copy(part).wait_send()
 
     @pl.when(core == 0)
     def _():
@@ -763,6 +859,9 @@
             pltpu.VMEM((NY, 16, QUARTER), F32),
             pltpu.VMEM((2, 4 * MODES, CHANNELS), BF16),
             pltpu.VMEM((16, CHANNELS), F32),
+            pltpu.VMEM((NY, 16, QUARTER), BF16),
+            pltpu.VMEM((NY, 16, QUARTER), BF16),
+            pltpu.VMEM((16, QUARTER), BF16),
             pltpu.VMEM((NY, 9, MODES, QUARTER), BF16),
             pltpu.VMEM((NY, 9, MODES, QUARTER), BF16),
             pltpu.VMEM((PLANE, 9, LANES), F32),
@@ -775,8 +874,8 @@
             pltpu.VMEM((9, LANES), F32),
             pltpu.SemaphoreType.DMA((4,)),
             pltpu.SemaphoreType.DMA((4,)),
-            pltpu.SemaphoreType.DMA((11,)),
-            pltpu.SemaphoreType.DMA((11,)),
+            pltpu.SemaphoreType.DMA((13,)),
+            pltpu.SemaphoreType.DMA((13,)),
         ],
         name="operator",
         compiler_params=pltpu.CompilerParams(

time: 54.9 us -> 51.8 us (0.944)
  Pallas kernels: 54 us -> 50.9 us
    pallas_call x1, Pallas kernels: 51.5 us -> 48.4 us  [shards(): pl.pallas_call(operator_kernel, out_shape=(block, block, block, block, ja...]
where the time goes in v4:
time: 51.8 us; the launch traced here: 51.6 us
  Pallas kernels  50.9 us (98%)
  between operations  0.64 us (1%)
    pallas_call x1, Pallas kernels, shards(): pl.pallas_call(operator_kernel, out_shape=(block, block, block, block, ja...  48.4 us
    pallas_call x1, Pallas kernels, shards(): pl.pallas_call(store_kernel, out_shape=tuple((jax.ShapeDtypeStruct(item.s...  2.48 us

profile of v4, /device:TPU:1, one launch (start us, length us, event | category | flops | bytes accessed | tf_op | source)
XLA Modules:
  0.0 51.6 jit_solution(4397536748200916990)
XLA Ops:
  0.6 48.4 %operator.1 = (bf16[128,2048]{1,0:T(8,128)(2,1)}, bf16[128,2048]{1,0:T(8,128)(2,1)}, bf16[128,2048]{1,0:T(8,128)(2,1)}, bf16[128,2048]{1,0:T(8,128)(2,1)}, f32[8,32]{1,0:T(8,128)}, /*index=5*/f32[3,3,2048]{2,1,0:T(4,128)}) custom-call(f32[8]{0:T(128)} %rate_ref.1, bf16[128,2048]{1,0:T(8,128)(2,1)} %bitcast.10, bf16[128,2048]{1,0:T(8,128)(2,1)} %bitcast.11, ...), custom_call_target="tpu_custom_call" | custom-call | tf_op jit(solution)/shard_map/operator/pallas_call | solution.py:826
  49.1 2.5 %store.1 = (bf16[128,2048]{1,0:T(8,128)(2,1)}, bf16[128,2048]{1,0:T(8,128)(2,1)}, bf16[128,2048]{1,0:T(8,128)(2,1)}, bf16[128,2048]{1,0:T(8,128)(2,1)}, f32[8,32]{1,0:T(8,128)}, /*index=5*/f32[3,3,2048]{2,1,0:T(4,128)}) custom-call(bf16[128,2048]{1,0:T(8,128)(2,1)} %get-tuple-element.18.refs_0_, bf16[128,2048]{1,0:T(8,128)(2,1)} %get-tuple-element.19.refs_1_, ...), custom_call_target="tpu_custom_call" | custom-call | tf_op jit(solution)/shard_map/store/pallas_call | solution.py:885

commit v5 on v4

--- a/solution.py
+++ b/solution.py
@@ -554,10 +554,6 @@
         b_send[other, 8:16] = finish
         finish = finish * step_decay + y_recv[other, 8:16]
 
-    for step in range(1, NY):
-        y_copy(b_send, b_recv, step, 2).start()
-    b_recv[y] = b_send[y]
-
     one = jnp.exp(-speeds)
     gains = jnp.sqrt(1.0 - jnp.exp(-2.0 * speeds))
     own_columns = residue_ref[:, mine] * gains
@@ -590,14 +586,18 @@
             device_id={"dp": peer},
             device_id_type=MESH,
         ).start()
+    for step in range(1, NY):
+        y_copy(b_send, b_recv, step, 2).start()
+    b_recv[y] = b_send[y]
+
     r_recv[dp] = r_send[dp]
+    settle(l_recv, PLANE - 1, 9)
+    total = l_recv[0]
+    for index in range(1, PLANE):
+        total = total + l_recv[index]
     settle(r_recv, NDP - 1, 3)
-    settle(l_recv, PLANE - 1, 9)
-    total = r_recv[0]
-    for index in range(1, NDP):
+    for index in range(NDP):
         total = total + r_recv[index]
-    for index in range(PLANE):
-        total = total + l_recv[index]
     p_send[...] = total
     p_recv[z] = total
 

time: 51.8 us -> 51.8 us (level)
  no operation moved by 1% of the time
where the time goes in v5:
time: 51.8 us; the launch traced here: 51.6 us
  Pallas kernels  50.9 us (98%)
  between operations  0.64 us (1%)
    pallas_call x1, Pallas kernels, shards(): pl.pallas_call(operator_kernel, out_shape=(block, block, block, block, ja...  48.4 us
    pallas_call x1, Pallas kernels, shards(): pl.pallas_call(store_kernel, out_shape=tuple((jax.ShapeDtypeStruct(item.s...  2.48 us

profile of v5, /device:TPU:1, one launch (start us, length us, event | category | flops | bytes accessed | tf_op | source)
XLA Modules:
  0.0 51.6 jit_solution(16875435416576092541)
XLA Ops:
  0.6 48.4 %operator.1 = (bf16[128,2048]{1,0:T(8,128)(2,1)}, bf16[128,2048]{1,0:T(8,128)(2,1)}, bf16[128,2048]{1,0:T(8,128)(2,1)}, bf16[128,2048]{1,0:T(8,128)(2,1)}, f32[8,32]{1,0:T(8,128)}, /*index=5*/f32[3,3,2048]{2,1,0:T(4,128)}) custom-call(f32[8]{0:T(128)} %rate_ref.1, bf16[128,2048]{1,0:T(8,128)(2,1)} %bitcast.10, bf16[128,2048]{1,0:T(8,128)(2,1)} %bitcast.11, ...), custom_call_target="tpu_custom_call" | custom-call | tf_op jit(solution)/shard_map/operator/pallas_call | solution.py:826
  49.1 2.5 %store.1 = (bf16[128,2048]{1,0:T(8,128)(2,1)}, bf16[128,2048]{1,0:T(8,128)(2,1)}, bf16[128,2048]{1,0:T(8,128)(2,1)}, bf16[128,2048]{1,0:T(8,128)(2,1)}, f32[8,32]{1,0:T(8,128)}, /*index=5*/f32[3,3,2048]{2,1,0:T(4,128)}) custom-call(bf16[128,2048]{1,0:T(8,128)(2,1)} %get-tuple-element.18.refs_0_, bf16[128,2048]{1,0:T(8,128)(2,1)} %get-tuple-element.19.refs_1_, ...), custom_call_target="tpu_custom_call" | custom-call | tf_op jit(solution)/shard_map/store/pallas_call | solution.py:885
